TPU v7x, 32 devices: a whole 2x2x4 slice. The times are simulated.
32 devices in a mesh: grp: 2 (over x), lon: 16 (over z, y, core), lat: 1.
Axes of the slice: x: 2, y: 2, z: 4, core: 2. Of those that a mesh axis runs over, the one named last changes fastest.
Arguments:
- tokens: bfloat16 [4, 8, 128, 1536], P('grp', 'lat', 'lon'), parts along dimension 0, may hold values from -6 to 6
- land: int32 [16, 128], P(('grp', 'lat'), 'lon'), parts along dimension 0, may hold values 0 or 1
- surface: float32 [2, 1536], replicated, may hold values from -4 to 4
- gain: float32 [1536], replicated, may hold values from 0.25 to 1.75
- weights: bfloat16 [1536, 3072], P('lon'), may hold values from -0.15625 to 0.15625
- shifts: int32 [2, 2], replicated, may hold values from 1 to 7, as said below
- index_table: int32 [64, 64], replicated, may hold values from 0 to 224
- bias_table: float32 [2, 225, 12], P('lat'), as said below
- cotangent: bfloat16 [4, 8, 128, 1536], P('grp', 'lat', 'lon'), parts along dimension 0, may hold values from -6 to 6
Outputs:
- output: bfloat16 [4, 8, 128, 1536], P('grp', 'lat', 'lon'), parts along dimension 0
- grad_tokens: bfloat16 [4, 8, 128, 1536], P('grp', 'lat', 'lon'), parts along dimension 0
- grad_weights: float32 [3072, 3072], P(('grp', 'lon')), parts along dimension 0
There are 2 independent parts, one for each index of `grp`. A program takes and returns all parts, laid end to end along the dimension named above; an argument that names none is the same for every part. Nothing has to cross between parts.
Inputs may be any that keep to these rules, and one draw needn't show every extreme that they name: `shifts`: row l holds level l's offsets along latitude and longitude; taken together the entries include 1 and 7. `bias_table`: every entry is finite.
All inputs are finite; a program needn't handle non-finite values. No bound on the sum of `land` on one device may be relied on, other than what follows from the above.
Results may differ from a plain program's by a relative error of at most 0.023.
Values may be sent and summed in bfloat16 or wider, within the bound.
A program may use at most 128 MiB of HBM per device.

v0:
```python
import math

import jax
import jax.numpy as jnp
from jax import lax
from jax.sharding import PartitionSpec as P

epsilon = 1e-05


def passed_along(shard, axis, by):
    count = lax.axis_size(axis)
    return lax.ppermute(shard, axis, [(i, (i + by) % count) for i in range(count)])


def normalize(stream, gain):
    values = stream.astype(jnp.float32)
    center = values - jnp.mean(values, axis=-1, keepdims=True)
    spread = lax.rsqrt(jnp.mean(center * center, axis=-1, keepdims=True) + epsilon)
    return (center * spread * gain).astype(jnp.bfloat16)


def normalize_back(stream, gain, grad_normed):
    values = stream.astype(jnp.float32)
    center = values - jnp.mean(values, axis=-1, keepdims=True)
    spread = lax.rsqrt(jnp.mean(center * center, axis=-1, keepdims=True) + epsilon)
    scaled = center * spread
    upstream = grad_normed.astype(jnp.float32) * gain
    return spread * (
        upstream
        - jnp.mean(upstream, axis=-1, keepdims=True)
        - scaled * jnp.mean(upstream * scaled, axis=-1, keepdims=True)
    )


def take_levels(field, starts, axis, length):

    def one_level(plane, start):
        return lax.dynamic_slice_in_dim(plane, start, length, axis - 1)

    return jax.vmap(one_level, in_axes=(1, 0), out_axes=1)(field, starts)


def roll_forward(field, shifts):
    tile_rows = field.shape[2]
    tile_cols = field.shape[3]
    below = passed_along(field, "lat", -1)
    rows_done = take_levels(jnp.concatenate([field, below], axis=2), shifts[:, 0], 2, tile_rows)
    beside = passed_along(rows_done, "lon", -1)
    return take_levels(jnp.concatenate([rows_done, beside], axis=3), shifts[:, 1], 3, tile_cols)


def roll_back(field, shifts):
    tile_rows = field.shape[2]
    tile_cols = field.shape[3]
    before = passed_along(field, "lon", 1)
    cols_done = take_levels(
        jnp.concatenate([before, field], axis=3), tile_rows - shifts[:, 1], 3, tile_cols
    )
    above = passed_along(cols_done, "lat", 1)
    return take_levels(
        jnp.concatenate([above, cols_done], axis=2), tile_rows - shifts[:, 0], 2, tile_rows
    )


def attend_forward(normed, w_qkv, w_out, bias_tile, allowed, heads):
    levels, tile_rows, tile_cols, model_width = normed.shape
    windows = tile_cols // tile_rows
    area = tile_rows * tile_rows
    qkv = jnp.dot(
        normed.reshape(-1, model_width), w_qkv, preferred_element_type=jnp.float32
    ).astype(jnp.bfloat16)
    view = qkv.reshape(levels, tile_rows, windows, tile_rows, 3, heads, -1)
    query = view[:, :, :, :, 0]
    keys = view[:, :, :, :, 1]
    values = view[:, :, :, :, 2]
    head_size = query.shape[-1]
    scale = 1.0 / math.sqrt(head_size)
    scores = jnp.einsum("lawbhd,lcwehd->lwhabce", query, keys, preferred_element_type=jnp.float32)
    scores = scores.reshape(levels, windows, heads, area, area) * scale + bias_tile[:, None]
    scores = jnp.where(allowed[:, None, None], scores, -1e30)
    top = jnp.max(scores, axis=-1, keepdims=True)
    expo = jnp.exp(scores - top)
    probs = expo / jnp.sum(expo, axis=-1, keepdims=True)
    probs_b = probs.astype(jnp.bfloat16).reshape(
        levels, windows, heads, tile_rows, tile_rows, tile_rows, tile_rows
    )
    mixed = jnp.einsum(
        "lwhabce,lcwehd->lawbhd", probs_b, values, preferred_element_type=jnp.float32
    )
    mixed_flat = mixed.astype(jnp.bfloat16).reshape(-1, heads * head_size)
    attended = lax.dot_general(
        mixed_flat, w_out, (((1,), (1,)), ((), ())), preferred_element_type=jnp.float32
    )
    attended = attended.astype(jnp.bfloat16).reshape(levels, tile_rows, tile_cols, model_width)
    return ((query, keys, values, probs, probs_b, mixed_flat), attended)


def attend_backward(rolled_cot, saved, w_qkv, w_out):
    query, keys, values, probs, probs_b, mixed_flat = saved
    levels, tile_rows, tile_cols, model_width = rolled_cot.shape
    heads = query.shape[4]
    head_size = query.shape[5]
    scale = 1.0 / math.sqrt(head_size)
    grad_mixed = jnp.dot(
        rolled_cot.reshape(-1, model_width), w_out, preferred_element_type=jnp.float32
    )
    grad_mixed = grad_mixed.astype(jnp.bfloat16).reshape(query.shape)
    grad_probs = jnp.einsum(
        "lawbhd,lcwehd->lwhabce", grad_mixed, values, preferred_element_type=jnp.float32
    )
    grad_probs = grad_probs.reshape(probs.shape)
    grad_values = jnp.einsum(
        "lwhabce,lawbhd->lcwehd", probs_b, grad_mixed, preferred_element_type=jnp.float32
    )
    grad_values = grad_values.astype(jnp.bfloat16)
    grad_scores = probs * (grad_probs - jnp.sum(probs * grad_probs, axis=-1, keepdims=True))
    grad_scores = (grad_scores * scale).astype(jnp.bfloat16).reshape(probs_b.shape)
    grad_query = jnp.einsum(
        "lwhabce,lcwehd->lawbhd", grad_scores, keys, preferred_element_type=jnp.float32
    )
    grad_keys = jnp.einsum(
        "lwhabce,lawbhd->lcwehd", grad_scores, query, preferred_element_type=jnp.float32
    )
    grad_qkv = jnp.stack(
        [grad_query.astype(jnp.bfloat16), grad_keys.astype(jnp.bfloat16), grad_values], axis=4
    )
    grad_qkv = grad_qkv.reshape(-1, 3 * heads * head_size)
    grad_normed = lax.dot_general(
        grad_qkv, w_qkv, (((1,), (1,)), ((), ())), preferred_element_type=jnp.float32
    )
    grad_normed = grad_normed.astype(jnp.bfloat16).reshape(
        levels, tile_rows, tile_cols, model_width
    )
    return (grad_normed, grad_qkv)


def on_device(tokens, land, surface, gain, weights, shifts, index_table, bias_table, cotangent):
    levels, tile_rows, tile_cols, model_width = tokens.shape
    heads = bias_table.shape[2]
    entries = bias_table.shape[1]
    proj_width = weights.shape[1] // 4
    full_weights = lax.all_gather(weights, "lon", axis=0, tiled=True)
    w_qkv = full_weights[:, : 3 * proj_width]
    w_out = full_weights[:, 3 * proj_width :]
    surface_term = jnp.where(land[None, :, :, None] == 1, surface[1], surface[0])
    stream = (tokens.astype(jnp.float32) + surface_term).astype(jnp.bfloat16)
    onehot = (index_table[:, :, None] == jnp.arange(entries, dtype=jnp.int32)).astype(jnp.float32)
    bias_tile = jnp.einsum("qkr,lrh->lhqk", onehot, bias_table, precision=lax.Precision.HIGHEST)
    total_rows = tile_rows * lax.axis_size("lat")
    row_number = lax.axis_index("lat") * tile_rows + jnp.arange(tile_rows, dtype=jnp.int32)
    group = row_number[None, :] >= (total_rows - shifts[:, 0])[:, None]
    group = jnp.repeat(group, tile_rows, axis=1)
    allowed = group[:, :, None] == group[:, None, :]
    normed = roll_forward(normalize(stream, gain)[None], shifts)[0]
    saved, attended = attend_forward(normed, w_qkv, w_out, bias_tile, allowed, heads)
    attended = roll_back(attended[None], shifts)[0]
    output = (stream.astype(jnp.float32) + attended.astype(jnp.float32)).astype(jnp.bfloat16)
    rolled_cot = roll_forward(cotangent[None], shifts)[0]
    grad_normed, grad_qkv = attend_backward(rolled_cot, saved, w_qkv, w_out)
    grad_normed = roll_back(grad_normed[None], shifts)[0]
    grad_stream = normalize_back(stream, gain, grad_normed)
    grad_tokens = (cotangent.astype(jnp.float32) + grad_stream).astype(jnp.bfloat16)
    flat_normed = normed.reshape(-1, model_width)
    flat_cot = rolled_cot.reshape(-1, model_width)
    mixed_flat = saved[5]
    first = lax.dot_general(
        flat_normed, grad_qkv, (((0,), (0,)), ((), ())), preferred_element_type=jnp.float32
    )
    second = lax.dot_general(
        flat_cot, mixed_flat, (((0,), (0,)), ((), ())), preferred_element_type=jnp.float32
    )
    grad_rows = lax.psum_scatter(
        jnp.concatenate([first, second], axis=1).astype(jnp.bfloat16),
        "lon",
        scatter_dimension=0,
        tiled=True,
    )
    summed = lax.psum(grad_rows, "lat").astype(jnp.float32)
    token_count = levels * tile_rows * lax.axis_size("lat") * tile_cols * lax.axis_size("lon")
    grad_weights = summed * (1.0 / math.sqrt(token_count))
    return (output, grad_tokens, grad_weights)


def solution(mesh):
    return jax.shard_map(
        on_device,
        mesh=mesh,
        in_specs=(
            P("grp", "lat", "lon", None),
            P(("grp", "lat"), "lon"),
            P(),
            P(),
            P("lon", None),
            P(),
            P(),
            P("lat", None, None),
            P("grp", "lat", "lon", None),
        ),
        out_specs=(
            P("grp", "lat", "lon", None),
            P("grp", "lat", "lon", None),
            P(("grp", "lon"), None),
        ),
        check_vma=False,
    )
```

profile of v0, /device:TPU:13, one launch (start us, length us, event | category | flops | bytes accessed | tf_op | source)
XLA Modules:
  0.0 314.1 jit_solution(16213481077203317431)
XLA Ops:
  16.5 6.0 %collective-permute-done.5 = bf16[1,2,8,8,1536]{4,3,2,1,0:T(8,128)(2,1)S(1)} collective-permute-done((bf16[1,2,8,8,1536]{4,3,2,1,0:T(8,128)(2,1)S(1)}, bf16[1,2,8,8,1536]{4,3,2,1,0:T(8,128)(2,1)S(1)}, u32[]{:S(2)}, u32[]{:S(2)}) %collective-permute-start.5) | collective-permute-done | bytes 393248 | tf_op jit(solution)/shard_map/ppermute | solution.py:13
  23.8 17.5 %collective-permute-done.1 = bf16[1,2,8,8,1536]{4,3,2,1,0:T(8,128)(2,1)S(1)} collective-permute-done((bf16[1,2,8,8,1536]{4,3,2,1,0:T(8,128)(2,1)S(1)}, bf16[1,2,8,8,1536]{4,3,2,1,0:T(8,128)(2,1)S(1)}, u32[]{:S(2)}, u32[]{:S(2)}) %collective-permute-start.1) | collective-permute-done | bytes 393248 | tf_op jit(solution)/shard_map/ppermute | solution.py:13
  42.5 55.0 %all-gather.2.cloned.1.call-done = bf16[1536,3072]{1,0:T(8,128)(2,1)} async-done(((bf16[96,3072]{1,0:T(8,128)(2,1)}), bf16[1536,3072]{1,0:T(8,128)(2,1)}) %all-gather.2.cloned.1.call-update) | async-done | bytes 9437200 | tf_op jit(solution)/shard_map/all_gather | solution.py:143
  100.0 4.3 %fusion.9 = bf16[128,2304]{1,0:T(8,128)(2,1)S(1)} fusion(bf16[128,1536]{1,0:T(8,128)(2,1)S(1)} %bitcast.157, bf16[1536,3072]{1,0:T(8,128)(2,1)} %all-gather.2.cloned.1.call-done), kind=kOutput, calls=%fused_computation.19 | convolution fusion | flops 906264576 | bytes 8060928 | tf_op jit(solution)/shard_map/dot_general | solution.py:70
  106.6 2.4 fusion.101
  109.0 3.8 %copy.96 = f32[2,12,8,8,8,8]{5,4,1,0,3,2:T(8,128)} copy(f32[2,12,8,8,8,8]{5,3,4,2,1,0:T(8,128)S(1)} %fusion.101) | data formatting | bytes 786432 | tf_op jit(solution)/shard_map/reshape | solution.py:112
  112.8 4.3 %reshape.232 = f32[2,12,64,64]{3,1,0,2:T(8,128)S(1)} reshape(f32[2,12,8,8,8,8]{5,4,1,0,3,2:T(8,128)} %copy.96) | data formatting | bytes 786432 | tf_op jit(solution)/shard_map/reshape | solution.py:112
  117.1 2.4 broadcast_multiply_fusion
  119.5 3.8 %copy.90 = f32[2,12,8,8,8,8]{5,4,1,0,3,2:T(8,128)} copy(f32[2,12,8,8,8,8]{5,3,4,2,1,0:T(8,128)S(1)} %broadcast_multiply_fusion) | data formatting | bytes 786432 | tf_op jit(solution)/shard_map/mul | solution.py:80
  123.3 4.3 %reshape.231 = f32[2,12,64,64]{3,1,0,2:T(8,128)S(1)} reshape(f32[2,12,8,8,8,8]{5,4,1,0,3,2:T(8,128)} %copy.90) | data formatting | bytes 786432 | tf_op jit(solution)/shard_map/mul | solution.py:80
  127.7 3.0 fusion.35
  130.7 21.7 %fusion.125 = (f32[2,12,64]{1,0,2:T(2,128)S(1)}, f32[2,12,64,64]{3,1,0,2:T(8,128)S(1)}) fusion(f32[2,12,64,64]{3,1,0,2:T(8,128)S(1)} %fusion.35), kind=kOutput, calls=%fused_computation.138 | output fusion | flops 196671 | bytes 792576 | tf_op jit(solution)/shard_map/sub | solution.py:83
  153.5 11.2 %fusion.53 = bf16[2,12,64,64]{3,1,0,2:T(8,128)(2,1)S(1)} fusion(f32[2,12,64,64]{3,1,0,2:T(8,128)S(1)} %reshape.232, f32[2,12,64,64]{3,1,0,2:T(8,128)S(1)} %get-tuple-element.26, f32[2,12,64]{1,0,2:T(2,128)S(1)} %get-tuple-element.25), kind=kOutput, calls=%fused_computation.48 | output fusion | flops 689727 | bytes 989184 | tf_op jit(solution)/shard_map/sub | solution.py:117
  165.6 3.5 %reshape.150 = bf16[2,12,8,8,8,8]{5,4,3,2,1,0:T(8,128)(2,1)S(1)} reshape(bf16[2,12,64,64]{3,2,1,0:T(8,128)(2,1)} %copy.65) | data formatting | bytes 393216 | tf_op jit(solution)/shard_map/reshape.30
  169.1 2.8 fusion.72
  171.9 2.3 fusion.69
  175.1 3.5 %reshape.146 = bf16[2,12,8,8,8,8]{5,4,3,2,1,0:T(8,128)(2,1)S(1)} reshape(bf16[2,12,64,64]{3,2,1,0:T(8,128)(2,1)} %copy.50) | data formatting | bytes 393216 | tf_op jit(solution)/shard_map/reshape.17
  178.6 2.8 fusion.75
  189.8 4.6 %pad_maximum_fusion = bf16[1536,3072]{1,0:T(8,128)(2,1)} fusion(bf16[1536,768]{1,0:T(8,128)(2,1)S(1)} %convolution_convert_fusion.1, bf16[1536,2304]{1,0:T(8,128)(2,1)S(1)} %convolution_convert_fusion), kind=kLoop, calls=%fused_computation.11 | loop fusion | flops 18874368 | bytes 18874368 | tf_op jit(solution)/shard_map/concatenate | solution.py:174
  194.5 5.5 %fusion.20 = bf16[128,1536]{1,0:T(8,128)(2,1)S(1)} fusion(bf16[128,2304]{1,0:T(8,128)(2,1)S(1)} %reshape.151, bf16[1536,3072]{1,0:T(8,128)(2,1)} %all-gather.2.cloned.1.call-done), kind=kOutput, calls=%fused_computation.30 | convolution fusion | flops 906166272 | bytes 8060928 | tf_op jit(solution)/shard_map/dot_general | solution.py:129
  202.2 2.9 convolution_convert_fusion.2
  207.7 3.5 %collective-permute-done.2 = bf16[1,2,8,8,1536]{4,2,1,3,0:T(8,128)(2,1)S(1)} collective-permute-done((bf16[1,2,8,8,1536]{4,2,1,3,0:T(8,128)(2,1)S(1)}, bf16[1,2,8,8,1536]{4,2,1,3,0:T(8,128)(2,1)S(1)}, u32[]{:S(2)}, u32[]{:S(2)}) %collective-permute-start.2) | collective-permute-done | bytes 393248 | tf_op jit(solution)/shard_map/ppermute | solution.py:13
  216.5 88.5 %reduce-scatter.2.cloned.1.call-done = bf16[96,3072]{1,0:T(8,128)(2,1)} async-done(((bf16[1536,3072]{1,0:T(8,128)(2,1)}), bf16[96,3072]{1,0:T(8,128)(2,1)}) %reduce-scatter.2.cloned.1.call-update) | async-done | bytes 589840 | tf_op jit(solution)/shard_map/reduce_scatter | solution.py:173
  305.0 2.2 convert_multiply_fusion
  (116 shorter events, 37.6 us)
Async XLA Ops:
  7.2 4.9 %copy-start.13 = (f32[1536]{0:T(1024)S(1)}, f32[1536]{0:T(1024)}, u32[]{:S(2)}) copy-start(f32[1536]{0:T(1024)} %param.12) | copy-start | bytes 18436
  7.2 5.3 %copy-start.19 = (s32[2,2]{1,0:T(2,128)S(1)}, s32[2,2]{1,0:T(2,128)}, u32[]{:S(2)}) copy-start(s32[2,2]{1,0:T(2,128)} %param.14) | copy-start | bytes 52
  7.2 90.3 %all-gather.2.cloned.1.call-start = ((), (), s32[]{:S(2)}) async-start(), calls=%async_computation.1 | async-start | bytes 10027008 | tf_op jit(solution)/shard_map/all_gather | solution.py:143
  7.9 297.1 %reduce-scatter.2.cloned.1.call-start = ((), (), s32[]{:S(2)}) async-start(), calls=%async_computation.2 | async-start | bytes 10027008 | tf_op jit(solution)/shard_map/reduce_scatter | solution.py:173
  9.0 4.6 %collective-permute-start.4 = (bf16[1,2,8,8,1536]{4,3,1,2,0:T(8,128)(2,1)S(1)}, bf16[1,2,8,8,1536]{4,3,1,2,0:T(8,128)(2,1)S(1)}, u32[]{:S(2)}, u32[]{:S(2)}) collective-permute-start(bf16[1,2,8,8,1536]{4,3,1,2,0:T(8,128)(2,1)S(1)} %bitcast.159), channel_id=1, source_target_pairs={{0,0},{1,1},{2,2},{3,3},{4,4},{5,5},{6,6},{7,7},{8,8},{9,9},{10,10... | collective-permute-start | bytes 1179656 | tf_op jit(solution)/shard_map/ppermute | solution.py:13
  12.4 2.6 collective-permute-start
  14.3 8.3 %collective-permute-start.5 = (bf16[1,2,8,8,1536]{4,3,2,1,0:T(8,128)(2,1)S(1)}, bf16[1,2,8,8,1536]{4,3,2,1,0:T(8,128)(2,1)S(1)}, u32[]{:S(2)}, u32[]{:S(2)}) collective-permute-start(bf16[1,2,8,8,1536]{4,3,2,1,0:T(8,128)(2,1)S(1)} %bitcast.161), channel_id=1, source_target_pairs={{0,15},{1,0},{2,1},{3,2},{4,3},{5,4},{6,5},{7,6},{8,7},{9,8},{10,9... | collective-permute-start | bytes 1179656 | tf_op jit(solution)/shard_map/ppermute | solution.py:13
  15.6 25.6 %collective-permute-start.1 = (bf16[1,2,8,8,1536]{4,3,2,1,0:T(8,128)(2,1)S(1)}, bf16[1,2,8,8,1536]{4,3,2,1,0:T(8,128)(2,1)S(1)}, u32[]{:S(2)}, u32[]{:S(2)}) collective-permute-start(bf16[1,2,8,8,1536]{4,3,2,1,0:T(8,128)(2,1)S(1)} %bitcast.163), channel_id=1, source_target_pairs={{0,15},{1,0},{2,1},{3,2},{4,3},{5,4},{6,5},{7,6},{8,7},{9,8},{10,9... | collective-permute-start | bytes 1179656 | tf_op jit(solution)/shard_map/ppermute | solution.py:13
  23.7 75.9 %copy-start.10 = (bf16[2,8,8,1536]{3,2,1,0:T(8,128)(2,1)}, bf16[2,8,8,1536]{3,2,1,0:T(8,128)(2,1)S(1)}, u32[]{:S(2)}) copy-start(bf16[2,8,8,1536]{3,2,1,0:T(8,128)(2,1)S(1)} %copy.60) | copy-start | bytes 1179652
  42.5 57.5 %copy-start.2 = (bf16[2,8,8,1536]{3,2,1,0:T(8,128)(2,1)}, bf16[2,8,8,1536]{3,2,1,0:T(8,128)(2,1)S(1)}, u32[]{:S(2)}) copy-start(bf16[2,8,8,1536]{3,2,1,0:T(8,128)(2,1)S(1)} %copy.42) | copy-start | bytes 1179652
  100.0 5.8 %copy-start = (bf16[2,8,8,12,64]{4,3,2,1,0:T(8,128)(2,1)}, bf16[2,8,8,12,64]{4,3,2,1,0:T(8,128)(2,1)S(1)}, u32[]{:S(2)}) copy-start(bf16[2,8,8,12,64]{4,3,2,1,0:T(8,128)(2,1)S(1)} %reshape.148) | copy-start | bytes 589828
  105.8 11.3 %copy-start.1 = (bf16[2,8,1,8,1,12,64]{6,5,4,3,1,0,2:T(8,128)(2,1)}, bf16[2,8,1,8,1,12,64]{6,5,4,3,1,0,2:T(8,128)(2,1)S(1)}, u32[]{:S(2)}) copy-start(bf16[2,8,1,8,1,12,64]{6,5,4,3,1,0,2:T(8,128)(2,1)S(1)} %get-tuple-element.21) | copy-start | bytes 589828
  105.8 11.3 %copy-start.7 = (bf16[2,8,1,8,1,12,64]{6,5,4,3,1,0,2:T(8,128)(2,1)}, bf16[2,8,1,8,1,12,64]{6,5,4,3,1,0,2:T(8,128)(2,1)S(1)}, u32[]{:S(2)}) copy-start(bf16[2,8,1,8,1,12,64]{6,5,4,3,1,0,2:T(8,128)(2,1)S(1)} %get-tuple-element.22) | copy-start | bytes 589828
  123.3 4.3 %copy-start.12 = (pred[2,64,64]{2,0,1:T(4,128)(4,1)S(1)}, pred[2,64,64]{2,0,1:T(4,128)(4,1)}, u32[]{:S(2)}) copy-start(pred[2,64,64]{2,0,1:T(4,128)(4,1)} %broadcast_compare_fusion) | copy-start | bytes 24580
  123.3 4.3 %copy-start.15 = (f32[2,225,12]{1,0,2:T(2,128)S(1)}, f32[2,225,12]{1,0,2:T(2,128)}, u32[]{:S(2)}) copy-start(f32[2,225,12]{1,0,2:T(2,128)} %param.16) | copy-start | bytes 64804
  123.3 4.3 %copy-start.16 = (s32[64,64]{1,0:T(8,128)S(1)}, s32[64,64]{1,0:T(8,128)}, u32[]{:S(2)}) copy-start(s32[64,64]{1,0:T(8,128)} %param.15) | copy-start | bytes 49156
  169.1 2.8 copy-start.8
  178.6 2.8 copy-start.6
  183.6 3.3 %copy-start.11 = (bf16[2,8,8,1536]{3,2,1,0:T(8,128)(2,1)S(1)}, bf16[2,8,8,1536]{3,2,1,0:T(8,128)(2,1)}, u32[]{:S(2)}) copy-start(bf16[2,8,8,1536]{3,2,1,0:T(8,128)(2,1)} %copy-done.10) | copy-start | bytes 1179652
  200.2 6.9 %copy-start.18 = (s32[2]{0:T(128)S(1)}, s32[2]{0:T(128)}, u32[]{:S(2)}) copy-start(s32[2]{0:T(128)} %get-tuple-element.17) | copy-start | bytes 28
  200.2 6.8 %collective-permute-start.6 = (bf16[1,2,8,8,1536]{4,2,1,3,0:T(8,128)(2,1)S(1)}, bf16[1,2,8,8,1536]{4,2,1,3,0:T(8,128)(2,1)S(1)}, u32[]{:S(2)}, u32[]{:S(2)}) collective-permute-start(bf16[1,2,8,8,1536]{4,2,1,3,0:T(8,128)(2,1)S(1)} %copy.71), channel_id=1, source_target_pairs={{0,1},{1,2},{2,3},{3,4},{4,5},{5,6},{6,7},{7,8},{8,9},{9,10},{10,1... | collective-permute-start | bytes 1179656 | tf_op jit(solution)/shard_map/ppermute | solution.py:13
  205.2 5.9 %collective-permute-start.2 = (bf16[1,2,8,8,1536]{4,2,1,3,0:T(8,128)(2,1)S(1)}, bf16[1,2,8,8,1536]{4,2,1,3,0:T(8,128)(2,1)S(1)}, u32[]{:S(2)}, u32[]{:S(2)}) collective-permute-start(bf16[1,2,8,8,1536]{4,2,1,3,0:T(8,128)(2,1)S(1)} %copy.53), channel_id=1, source_target_pairs={{0,1},{1,2},{2,3},{3,4},{4,5},{5,6},{6,7},{7,8},{8,9},{9,10},{10,1... | collective-permute-start | bytes 1179656 | tf_op jit(solution)/shard_map/ppermute | solution.py:13
  207.6 4.3 %collective-permute-start.7 = (bf16[1,2,8,8,1536]{4,2,3,1,0:T(8,128)(2,1)S(1)}, bf16[1,2,8,8,1536]{4,2,3,1,0:T(8,128)(2,1)S(1)}, u32[]{:S(2)}, u32[]{:S(2)}) collective-permute-start(bf16[1,2,8,8,1536]{4,2,3,1,0:T(8,128)(2,1)S(1)} %bitcast.165), channel_id=1, source_target_pairs={{0,0},{1,1},{2,2},{3,3},{4,4},{5,5},{6,6},{7,7},{8,8},{9,9},{10,10... | collective-permute-start | bytes 1179656 | tf_op jit(solution)/shard_map/ppermute | solution.py:13
  211.8 0.6 collective-permute-start.3
  (6 other events, 10.3 us)
Sparse Core Ops, SparseCore 0:
  10.3 87.1 all-gather.1
  194.6 110.3 reduce-scatter.1
where the time goes:
time: 317 us; the launch traced here: 314 us
  waiting for transfers between devices  173 us (55%)
  other arithmetic  47.9 us (15%)
  local copies, waits for them, and re-layouts  40.4 us (13%)
  matrix products  35 us (11%)
  between operations  14.7 us (5%)
  starting transfers between devices  3.37 us (1%)
    reduce_scatter x1, waiting for transfers between devices, on_device(): lax.psum_scatter(jnp.concatenate([first, second], axis=1).astype(jnp.bflo...  88.5 us
    all_gather x1, waiting for transfers between devices, on_device(): full_weights = lax.all_gather(weights, 'lon', axis=0, tiled=True)  55 us
    ppermute x8, waiting for transfers between devices, passed_along(): lax.ppermute(shard, axis, [(i, (i + by) % count) for i in range(count)])  28.5 us
    sub x1, other arithmetic, attend_forward(): expo = jnp.exp(scores - top)  21.7 us
    sub x1, other arithmetic, attend_backward(): grad_probs - jnp.sum(probs * grad_probs, axis=-1, keepdims=True)  11.2 us
    mul x2, local copies, waits for them, and re-layouts, attend_forward(): scores.reshape(levels, windows, heads, area, area) * scale  8.12 us
    reshape x2, local copies, waits for them, and re-layouts, attend_backward(): grad_probs = grad_probs.reshape(probs.shape)  8.11 us
    another operation x3, local copies, waits for them, and re-layouts  7.23 us
  transfers between devices with their start and end apart: 10, of which 6 were waited for; matrix products, arithmetic and copies ran while one was open for 8% of the time, Pallas kernels for 0%

commit v1 on v0

v1 whole, which is shorter than its diff:
```python
import functools
import math

import jax
import jax.numpy as jnp
from jax import lax
from jax.experimental import pallas as pl
from jax.experimental.pallas import tpu as pltpu
from jax.sharding import PartitionSpec as P

epsilon = 1e-05
f32 = jnp.float32
bf16 = jnp.bfloat16
VMEM = pl.BlockSpec(memory_space=pltpu.VMEM)


def passed_along(shard, axis, by):
    count = lax.axis_size(axis)
    return lax.ppermute(shard, axis, [(i, (i + by) % count) for i in range(count)])


def dot(a, b, dims):
    return lax.dot_general(a, b, ((dims[0], dims[1]), ((), ())), preferred_element_type=f32)


def normalize(stream, gain):
    values = stream.astype(f32)
    center = values - jnp.mean(values, axis=-1, keepdims=True)
    spread = lax.rsqrt(jnp.mean(center * center, axis=-1, keepdims=True) + epsilon)
    return (center * spread * gain).astype(bf16)


def normalize_back(stream, gain, grad_normed):
    values = stream.astype(f32)
    center = values - jnp.mean(values, axis=-1, keepdims=True)
    spread = lax.rsqrt(jnp.mean(center * center, axis=-1, keepdims=True) + epsilon)
    scaled = center * spread
    upstream = grad_normed.astype(f32) * gain
    return spread * (
        upstream
        - jnp.mean(upstream, axis=-1, keepdims=True)
        - scaled * jnp.mean(upstream * scaled, axis=-1, keepdims=True)
    )


def take_levels(field, starts, axis, length):

    def one_level(plane, start):
        return lax.dynamic_slice_in_dim(plane, start, length, axis - 1)

    return jax.vmap(one_level, in_axes=(1, 0), out_axes=1)(field, starts)


def attend_kernel(width, p_own, p_east, mine, east, w, bias, rolled, qkvm, grads, dw, proj):
    tokens, model = rolled.shape[1:]
    for part in range(2):
        def roll_tile(t, _):
            cols = pl.ds(pl.multiple_of(t * 512, 512), 512)
            moved = dot(p_own[...], mine[part, :, cols], ((1,), (0,)))
            moved += dot(p_east[...], east[part, :, cols], ((1,), (0,)))
            rolled[part, :, cols] = moved.astype(bf16)
            return 0
        lax.fori_loop(0, model // 512, roll_tile, 0)

    def proj_tile(src):
        def body(t, _):
            cols = pl.ds(pl.multiple_of(t * 256, 256), 256)
            proj[:, cols] = dot(rolled[src], w[:, cols], ((1,), (0,))).astype(bf16)
            return 0
        return body

    lax.fori_loop(0, 3 * width // 256, proj_tile(0), 0)
    lax.fori_loop(3 * width // 256, 4 * width // 256, proj_tile(1), 0)

    left = lax.broadcasted_iota(jnp.int32, (tokens, 128), 1) < 64
    scale = 0.125

    def pair(j, _):
        def cols(block):
            return pl.ds(pl.multiple_of(block * width + j * 128, 128), 128)
        q, k, v, g = (proj[:, cols(b)] for b in range(4))
        outs = []
        for half in range(2):
            keep = left if half == 0 else jnp.logical_not(left)
            zero = jnp.zeros_like(q)
            s = dot(jnp.where(keep, q, zero), k, ((1,), (1,))) * scale + bias[2 * j + half]
            top = jnp.max(s, axis=-1, keepdims=True)
            expo = jnp.exp(s - top)
            probs = expo / jnp.sum(expo, axis=-1, keepdims=True)
            probs_b = probs.astype(bf16)
            mixed = dot(probs_b, v, ((1,), (0,)))
            grad_probs = dot(jnp.where(keep, g, zero), v, ((1,), (1,)))
            grad_v = dot(probs_b, g, ((0,), (0,)))
            inner = jnp.sum(probs * grad_probs, axis=-1, keepdims=True)
            gs = (probs * (grad_probs - inner) * scale).astype(bf16)
            outs.append((mixed, dot(gs, k, ((1,), (0,))), dot(gs, q, ((0,), (0,))), grad_v))
        mixed, grad_q, grad_k, grad_v = (jnp.where(left, a, b).astype(bf16) for a, b in zip(*outs))
        grads[:, cols(0)] = grad_q
        grads[:, cols(1)] = grad_k
        grads[:, cols(2)] = grad_v
        grads[:, cols(3)] = mixed
        return 0

    lax.fori_loop(0, width // 128, pair, 0)

    def weight_tile(t, _):
        rows = pl.ds(pl.multiple_of(t * 128, 128), 128)
        first = dot(rolled[0, :, rows], grads[:, : 3 * width], ((0,), (0,)))
        dw[rows, : 3 * width] = first.astype(bf16)
        second = dot(rolled[1, :, rows], grads[:, 3 * width :], ((0,), (0,)))
        dw[rows, 3 * width :] = second.astype(bf16)
        return 0

    lax.fori_loop(0, model // 128, weight_tile, 0)


def project_kernel(width, p_own, p_east, grads, w, keep, send):
    model = w.shape[0]

    def body(t, _):
        rows = pl.ds(pl.multiple_of(t * 256, 256), 256)
        attended = dot(grads[:, 3 * width :], w[rows, 3 * width :], ((1,), (1,))).astype(bf16)
        grad_normed = dot(grads[:, : 3 * width], w[rows, : 3 * width], ((1,), (1,))).astype(bf16)
        for part, field in enumerate((attended, grad_normed)):
            keep[part, :, rows] = dot(p_own[...], field, ((0,), (0,))).astype(bf16)
            send[part, :, rows] = dot(p_east[...], field, ((0,), (0,))).astype(bf16)
        return 0

    lax.fori_loop(0, model // 256, body, 0)


def on_device(tokens, land, surface, gain, weights, shifts, index_table, bias_table, cotangent):
    levels, tile_rows, tile_cols, model = tokens.shape
    heads = bias_table.shape[2]
    entries = bias_table.shape[1]
    width = weights.shape[1] // 4
    count = levels * tile_rows * tile_cols
    area = tile_rows * tile_rows
    lats = lax.axis_size("lat")
    w = lax.all_gather(weights, "lon", axis=0, tiled=True)

    surface_term = jnp.where(land[None, :, :, None] == 1, surface[1], surface[0])
    stream = (tokens.astype(f32) + surface_term).astype(bf16)
    fields = jnp.stack([normalize(stream, gain), cotangent])
    row_shift = shifts[:, 0]
    if lats > 1:
        below = passed_along(fields, "lat", -1)
        both = jnp.concatenate([fields, below], axis=2)
        fields = jax.vmap(lambda f: take_levels(f[None], row_shift, 2, tile_rows)[0])(both)
        row_shift = jnp.zeros_like(row_shift)
    mine = fields.reshape(2, count, model)
    east = passed_along(mine, "lon", -1)

    cell = jnp.arange(count, dtype=jnp.int32)
    lev, row, col = cell // (tile_rows * tile_cols), cell // tile_cols % tile_rows, cell % tile_cols
    from_row = (row + row_shift[lev]) % tile_rows
    from_col = col + shifts[lev, 1]
    source = lev * tile_rows * tile_cols + from_row * tile_cols + from_col % tile_cols
    hit = source[:, None] == cell[None, :]
    inside = (from_col < tile_cols)[:, None]
    p_own = jnp.where(hit & inside, 1.0, 0.0).astype(bf16)
    p_east = jnp.where(hit & ~inside, 1.0, 0.0).astype(bf16)

    onehot = (index_table[:, :, None] == jnp.arange(entries, dtype=jnp.int32)).astype(f32)
    bias = jnp.einsum("qkr,lrh->hlqk", onehot, bias_table, precision=lax.Precision.HIGHEST)
    total_rows = tile_rows * lats
    row_number = lax.axis_index("lat") * tile_rows + jnp.arange(tile_rows, dtype=jnp.int32)
    group = row_number[None, :] >= (total_rows - shifts[:, 0])[:, None]
    group = jnp.repeat(group, tile_rows, axis=1)
    allowed = group[:, :, None] == group[:, None, :]
    bias = jnp.where(allowed[None], bias, -1e30)
    other = jnp.full((heads, area, area), -jnp.inf, f32)
    bias = jnp.concatenate(
        [jnp.concatenate([bias[:, 0], other], axis=2), jnp.concatenate([other, bias[:, 1]], axis=2)],
        axis=1,
    )

    params = pltpu.CompilerParams(vmem_limit_bytes=56 * 2**20)
    grads, dw = pl.pallas_call(
        lambda a, b, c, d, e, f, g, h, r, p: attend_kernel(width, a, b, c, d, e, f, r, None, g, h, p),
        name="attend",
        out_shape=(
            jax.ShapeDtypeStruct((count, 4 * width), bf16),
            jax.ShapeDtypeStruct((model, 4 * width), bf16),
        ),
        in_specs=[VMEM] * 6,
        out_specs=(VMEM, VMEM),
        scratch_shapes=[pltpu.VMEM((2, count, model), bf16), pltpu.VMEM((count, 4 * width), bf16)],
        compiler_params=params,
        cost_estimate=pl.CostEstimate(flops=3 * 10**9, bytes_accessed=24 * 10**6, transcendentals=200000),
    )(p_own, p_east, mine, east, w, bias)
    summed = lax.psum_scatter(dw, "lon", scatter_dimension=0, tiled=True)
    keep, send = pl.pallas_call(
        functools.partial(project_kernel, width),
        name="project",
        out_shape=(jax.ShapeDtypeStruct((2, count, model), bf16),) * 2,
        in_specs=[VMEM] * 4,
        out_specs=(VMEM, VMEM),
        compiler_params=params,
        cost_estimate=pl.CostEstimate(flops=2 * 10**9, bytes_accessed=13 * 10**6, transcendentals=0),
    )(p_own, p_east, grads, w)
    west = passed_along(send, "lon", 1)
    back = (keep.astype(f32) + west.astype(f32)).astype(bf16)
    back = back.reshape(2, levels, tile_rows, tile_cols, model)
    if lats > 1:
        above = passed_along(back, "lat", 1)
        both = jnp.concatenate([above, back], axis=2)
        starts = tile_rows - shifts[:, 0]
        back = jax.vmap(lambda f: take_levels(f[None], starts, 2, tile_rows)[0])(both)
    output = (stream.astype(f32) + back[0].astype(f32)).astype(bf16)
    grad_stream = normalize_back(stream, gain, back[1])
    grad_tokens = (cotangent.astype(f32) + grad_stream).astype(bf16)
    summed = lax.psum(summed, "lat").astype(f32)
    token_count = count * lats * lax.axis_size("lon")
    grad_weights = summed * (1.0 / math.sqrt(token_count))
    return (output, grad_tokens, grad_weights)


def solution(mesh):
    return jax.shard_map(
        on_device,
        mesh=mesh,
        in_specs=(
            P("grp", "lat", "lon", None),
            P(("grp", "lat"), "lon"),
            P(),
            P(),
            P("lon", None),
            P(),
            P(),
            P("lat", None, None),
            P("grp", "lat", "lon", None),
        ),
        out_specs=(
            P("grp", "lat", "lon", None),
            P("grp", "lat", "lon", None),
            P(("grp", "lon"), None),
        ),
        check_vma=False,
    )
```

time: 317 us -> 242 us (0.76)
  local copies, waits for them, and re-layouts: 40.4 us -> 3.2 us
  Pallas kernels: 0 us -> 36.2 us
  other arithmetic: 47.9 us -> 12.1 us
  matrix products: 35 us -> 3 us
  waiting for transfers between devices: 173 us -> 168 us
    pallas_call x0 -> x2, Pallas kernels: none -> 36.2 us  [the longest x1 25.6 us: on_device(): pl.pallas_call(lambda a, b, c, d, e, f, g, h, r, p: attend_kernel(width,...]
    sub x2 -> x1, other arithmetic: 32.9 us -> 0.12 us  [on_device(): group = row_number[None, :] >= (total_rows - shifts[:, 0])[:, None]]
    dot_general x13 -> x1, matrix products: 35 us -> 3 us  [on_device(): jnp.einsum('qkr,lrh->hlqk', onehot, bias_table, precision=lax.Precision.H...]
    ppermute x8 -> x2, waiting for transfers between devices: 28.5 us -> 15.7 us  [passed_along(): lax.ppermute(shard, axis, [(i, (i + by) % count) for i in range(count)])]
    all_gather x1, waiting for transfers between devices: 55 us -> 66.7 us  [on_device(): w = lax.all_gather(weights, 'lon', axis=0, tiled=True)]
    reshape x5 -> x0, local copies, waits for them, and re-layouts: 10.5 us -> none  [the longest x2 8.11 us: attend_backward(): grad_probs = grad_probs.reshape(probs.shape)]
    another operation x6 -> x0, local copies, waits for them, and re-layouts: 8.28 us -> none
    mul x2 -> x0, local copies, waits for them, and re-layouts: 8.12 us -> none  [attend_forward(): scores.reshape(levels, windows, heads, area, area) * scale]
  transfers between devices with their start and end apart: 10 -> 4, of which waited for: 6 -> 4; matrix products, arithmetic and copies ran while one was open for 8% -> 7% of each run, Pallas kernels for 0% -> 4%
where the time goes in v1:
time: 242 us; the launch traced here: 240 us
  waiting for transfers between devices  168 us (69%)
  Pallas kernels  36.2 us (15%)
  between operations  14.2 us (6%)
  other arithmetic  12.1 us (5%)
  local copies, waits for them, and re-layouts  3.2 us (1%)
  matrix products  3 us (1%)
  starting transfers between devices  2.82 us (1%)
    reduce_scatter x1, waiting for transfers between devices, on_device(): summed = lax.psum_scatter(dw, 'lon', scatter_dimension=0, tiled=True)  85.3 us
    all_gather x1, waiting for transfers between devices, on_device(): w = lax.all_gather(weights, 'lon', axis=0, tiled=True)  66.7 us
    pallas_call x1, Pallas kernels, on_device(): pl.pallas_call(lambda a, b, c, d, e, f, g, h, r, p: attend_kernel(width,...  25.6 us
    ppermute x2, waiting for transfers between devices, passed_along(): lax.ppermute(shard, axis, [(i, (i + by) % count) for i in range(count)])  15.7 us
    pallas_call x1, Pallas kernels, on_device(): pl.pallas_call(functools.partial(project_kernel, width), name='project',...  10.5 us
  transfers between devices with their start and end apart: 4, of which 4 were waited for; matrix products, arithmetic and copies ran while one was open for 7% of the time, Pallas kernels for 4%

profile of v1, /device:TPU:13, one launch (start us, length us, event | category | flops | bytes accessed | tf_op | source)
XLA Modules:
  0.0 239.9 jit_solution(2607274275399246879)
XLA Ops:
  7.2 0.7 all-gather.2.cloned.1.call-update
  8.0 0.8 slice_reduce_fusion.1
  8.8 0.7 broadcast_compare_fusion.1
  9.6 1.2 convert_reduce_fusion
  11.0 0.3 fusion.9
  11.4 0.7 collective-permute-start
  12.2 1.5 gather_fusion
  14.2 3.0 %fusion.1 = f32[64,64,2,12]{1,3,2,0:T(8,128)S(1)} fusion(s32[64,64]{1,0:T(8,128)S(1)} %copy-done.5, f32[2,225,12]{1,0,2:T(2,128)S(1)} %copy-done.6), kind=kOutput, calls=%fused_computation.3 | convolution fusion | flops 266342400 | bytes 431200 | tf_op jit(solution)/shard_map/qkr,lrh->hlqk/dot_general | solution.py:165
  17.2 0.5 bitcast_select_fusion
  17.8 1.1 pad_maximum_fusion.f
  18.9 0.5 fusion.33
  19.4 1.3 fusion.23
  20.7 0.7 select_convert_fusion
  21.5 6.5 %collective-permute-done.d = bf16[2,128,1536]{2,1,0:T(8,128)(2,1)S(1)} collective-permute-done((bf16[2,128,1536]{2,1,0:T(8,128)(2,1)S(1)}, bf16[2,128,1536]{2,1,0:T(8,128)(2,1)S(1)}, u32[]{:S(2)}, u32[]{:S(2)}) %collective-permute-start) | collective-permute-done | bytes 786464 | tf_op jit(solution)/shard_map/ppermute | solution.py:19
  27.9 66.7 %all-gather.2.cloned.1.call-done.e.w = bf16[1536,3072]{1,0:T(8,128)(2,1)} async-done(((bf16[96,3072]{1,0:T(8,128)(2,1)}), bf16[1536,3072]{1,0:T(8,128)(2,1)}) %all-gather.2.cloned.1.call-update) | async-done | bytes 9437200 | tf_op jit(solution)/shard_map/all_gather | solution.py:140
  94.6 25.6 %attend.1 = (bf16[128,3072]{1,0:T(8,128)(2,1)}, bf16[1536,3072]{1,0:T(8,128)(2,1)}) custom-call(bf16[128,128]{1,0:T(8,128)(2,1)} %get-tuple-element.26.a.p_own, bf16[128,128]{1,0:T(8,128)(2,1)} %get-tuple-element.25.b.p_east, bf16[2,128,1536]{2,1,0:T(8,128)(2,1)} %copy-done.1, bf16[2,128,1536]{2,1,0:T(8,128)(2,1)} %copy-done.3, ...), custom_call_target="tpu_custom_call" | custom-call | flops 3000000000 | bytes 24000000 | tf_op jit(solution)/shard_map/attend/pallas_call | solution.py:179
  120.3 10.5 %project.1 = (bf16[2,128,1536]{2,1,0:T(8,128)(2,1)}, bf16[2,128,1536]{2,1,0:T(8,128)(2,1)}) custom-call(bf16[128,128]{1,0:T(8,128)(2,1)} %get-tuple-element.26.a.p_own, bf16[128,128]{1,0:T(8,128)(2,1)} %get-tuple-element.25.b.p_east, bf16[128,3072]{1,0:T(8,128)(2,1)} %get-tuple-element.7.grads, bf16[1536,3072]{1,0:T(8,128)(2,1)} %all-gather.2.cloned.1.call-done.e.w), custom_call_target="tpu_custom_call" | custom-call | flops 2000000000 | bytes 13000000 | tf_op jit(solution)/shard_map/project/pallas_call | solution.py:193
  130.8 2.0 collective-permute-start.1
  132.9 9.3 %collective-permute-done.1 = bf16[2,128,1536]{2,1,0:T(8,128)(2,1)S(1)} collective-permute-done((bf16[2,128,1536]{2,1,0:T(8,128)(2,1)}, bf16[2,128,1536]{2,1,0:T(8,128)(2,1)S(1)}, u32[]{:S(2)}, u32[]{:S(2)}) %collective-permute-start.1) | collective-permute-done | bytes 786464 | tf_op jit(solution)/shard_map/ppermute | solution.py:19
  142.1 1.4 add_convert_fusion
  143.8 0.3 fusion.10
  144.2 1.4 fusion.14
  145.5 85.3 %reduce-scatter.2.cloned.1.call-done = bf16[96,3072]{1,0:T(8,128)(2,1)} async-done(((bf16[1536,3072]{1,0:T(8,128)(2,1)}), bf16[96,3072]{1,0:T(8,128)(2,1)}) %reduce-scatter.2.cloned.1.call-update) | async-done | bytes 589840 | tf_op jit(solution)/shard_map/reduce_scatter | solution.py:192
  230.8 2.2 convert_multiply_fusion
  (36 shorter events, 1.5 us)
Async XLA Ops:
  7.2 3.9 %copy-start.4 = (f32[1536]{0:T(1024)S(1)}, f32[1536]{0:T(1024)}, u32[]{:S(2)}) copy-start(f32[1536]{0:T(1024)} %param.12) | copy-start | bytes 18436
  7.2 87.5 %all-gather.2.cloned.1.call-start = ((), (), s32[]{:S(2)}) async-start(), calls=%async_computation.1 | async-start | bytes 10027008 | tf_op jit(solution)/shard_map/all_gather | solution.py:140
  7.9 3.4 %copy-start.2 = (bf16[2,8,8,1536]{3,2,1,0:T(8,128)(2,1)S(1)}, bf16[2,8,8,1536]{3,2,1,0:T(8,128)(2,1)}, u32[]{:S(2)}) copy-start(bf16[2,8,8,1536]{3,2,1,0:T(8,128)(2,1)} %param.17) | copy-start | bytes 1179652
  7.9 222.9 %reduce-scatter.2.cloned.1.call-start = ((), (), s32[]{:S(2)}) async-start(), calls=%async_computation.2 | async-start | bytes 10027008 | tf_op jit(solution)/shard_map/reduce_scatter | solution.py:192
  10.8 1.4 copy-start
  11.0 3.2 %copy-start.5 = (s32[64,64]{1,0:T(8,128)S(1)}, s32[64,64]{1,0:T(8,128)}, u32[]{:S(2)}) copy-start(s32[64,64]{1,0:T(8,128)} %param.15) | copy-start | bytes 49156
  11.0 3.2 %copy-start.6 = (f32[2,225,12]{1,0,2:T(2,128)S(1)}, f32[2,225,12]{1,0,2:T(2,128)}, u32[]{:S(2)}) copy-start(f32[2,225,12]{1,0,2:T(2,128)} %param.16) | copy-start | bytes 64804
  11.4 6.3 %copy-start.1 = (bf16[2,128,1536]{2,1,0:T(8,128)(2,1)}, bf16[2,128,1536]{2,1,0:T(8,128)(2,1)S(1)}, u32[]{:S(2)}) copy-start(bf16[2,128,1536]{2,1,0:T(8,128)(2,1)S(1)} %pad_maximum_fusion.1.c) | copy-start | bytes 2359300
  11.4 16.5 %collective-permute-start = (bf16[2,128,1536]{2,1,0:T(8,128)(2,1)S(1)}, bf16[2,128,1536]{2,1,0:T(8,128)(2,1)S(1)}, u32[]{:S(2)}, u32[]{:S(2)}) collective-permute-start(bf16[2,128,1536]{2,1,0:T(8,128)(2,1)S(1)} %pad_maximum_fusion.1.c), channel_id=1, source_target_pairs={{0,15},{1,0},{2,1},{3,2},{4,3},{5,4},{6,5},{7,6},{8,7},{9,8},{10,9... | collective-permute-start | bytes 2359304 | tf_op jit(solution)/shard_map/ppermute | solution.py:19
  27.9 66.7 %copy-start.3 = (bf16[2,128,1536]{2,1,0:T(8,128)(2,1)}, bf16[2,128,1536]{2,1,0:T(8,128)(2,1)S(1)}, u32[]{:S(2)}) copy-start(bf16[2,128,1536]{2,1,0:T(8,128)(2,1)S(1)} %collective-permute-done.d) | copy-start | bytes 2359300
  130.8 11.3 %collective-permute-start.1 = (bf16[2,128,1536]{2,1,0:T(8,128)(2,1)}, bf16[2,128,1536]{2,1,0:T(8,128)(2,1)S(1)}, u32[]{:S(2)}, u32[]{:S(2)}) collective-permute-start(bf16[2,128,1536]{2,1,0:T(8,128)(2,1)} %get-tuple-element.9), channel_id=1, source_target_pairs={{0,1},{1,2},{2,3},{3,4},{4,5},{5,6},{6,7},{7,8},{8,9},{9,10},{10,1... | collective-permute-start | bytes 2359304 | tf_op jit(solution)/shard_map/ppermute | solution.py:19
Sparse Core Ops, SparseCore 0:
  10.3 84.3 all-gather.1
  120.4 110.3 reduce-scatter.1

commit v2 on v1

--- a/solution.py
+++ b/solution.py
@@ -11,6 +11,8 @@
 epsilon = 1e-05
 f32 = jnp.float32
 bf16 = jnp.bfloat16
+MESH = pl.DeviceIdType.MESH
+ANY = pl.BlockSpec(memory_space=pl.ANY)
 VMEM = pl.BlockSpec(memory_space=pltpu.VMEM)
 
 
@@ -51,7 +53,7 @@
     return jax.vmap(one_level, in_axes=(1, 0), out_axes=1)(field, starts)
 
 
-def attend_kernel(width, p_own, p_east, mine, east, w, bias, rolled, qkvm, grads, dw, proj):
+def attend_kernel(width, p_own, p_east, mine, east, w, bias, grads, rolled_t, rolled, proj):
     tokens, model = rolled.shape[1:]
     for part in range(2):
         def roll_tile(t, _):
@@ -59,6 +61,7 @@
             moved = dot(p_own[...], mine[part, :, cols], ((1,), (0,)))
             moved += dot(p_east[...], east[part, :, cols], ((1,), (0,)))
             rolled[part, :, cols] = moved.astype(bf16)
+            rolled_t[part, cols, :] = moved.T.astype(bf16)
             return 0
         lax.fori_loop(0, model // 512, roll_tile, 0)
 
@@ -103,21 +106,188 @@
 
     lax.fori_loop(0, width // 128, pair, 0)
 
-    def weight_tile(t, _):
-        rows = pl.ds(pl.multiple_of(t * 128, 128), 128)
-        first = dot(rolled[0, :, rows], grads[:, : 3 * width], ((0,), (0,)))
-        dw[rows, : 3 * width] = first.astype(bf16)
-        second = dot(rolled[1, :, rows], grads[:, 3 * width :], ((0,), (0,)))
-        dw[rows, 3 * width :] = second.astype(bf16)
+
+def where_am_i():
+    me = lax.axis_index("lon")
+    return me, me // 4, me // 2 % 2, me % 2
+
+
+def index_of(z, y, c):
+    return (z * 2 + y) * 2 + c
+
+
+def signal(barrier, **where):
+    pl.semaphore_signal(barrier, inc=1, device_id=where, device_id_type=MESH)
+
+
+def line_neighbours(z, last):
+    return (z + last) // (last + 1) + (2 * last - z) // (last + 1)
+
+
+def gather_kernel(n, shard, full, local_sem, send_sem, recv_sem):
+    me, z, y, c = where_am_i()
+    x = lax.axis_index("grp")
+    last = n // 4 - 1
+    barrier = pltpu.get_barrier_semaphore()
+    signal(barrier, grp=1 - x)
+    signal(barrier, lon=index_of(z, y, 1 - c))
+    signal(barrier, lon=index_of(z, 1 - y, c))
+    pl.when(z > 0)(lambda: signal(barrier, lon=me - 4))
+    pl.when(z < last)(lambda: signal(barrier, lon=me + 4))
+    pl.semaphore_wait(barrier, 3 + line_neighbours(z, last))
+
+    def whole(j, way, where, src=None):
+        return pltpu.make_async_remote_copy(
+            full.at[j] if src is None else src, full.at[j],
+            send_sem.at[j, way, 0], recv_sem.at[j, 0], device_id=where, device_id_type=MESH)
+
+    def half(j, h, way, where, src=None):
+        return pltpu.make_async_remote_copy(
+            full.at[j, h] if src is None else src, full.at[j, h],
+            send_sem.at[j, way, h], recv_sem.at[j, h], device_id=where, device_id_type=MESH)
+
+    partner = {"lon": index_of(z, y, 1 - c)}
+    across = {"lon": index_of(z, 1 - y, c)}
+    right, left, peer = {"lon": me + 4}, {"lon": me - 4}, {"grp": 1 - x}
+
+    def spread(j, act, src=None, to_right=True, to_left=True):
+        if to_right:
+            pl.when(z < last)(lambda: act(whole(j, 0, right, src)))
+        if to_left:
+            pl.when(z > 0)(lambda: act(whole(j, 1, left, src)))
+        act(half(j, x, 2, across, None if src is None else src.at[x]))
+        act(whole(j, 3, partner, src))
+
+    def own_column(t, act):
+        def from_left():
+            act(me - 4 * t, dict(to_left=False))
+        def from_right():
+            act(me + 4 * t, dict(to_right=False))
+        pl.when(z - t >= 0)(from_left)
+        pl.when(z + t <= last)(from_right)
+
+    def other_column(t, act):
+        base = index_of(z, 1 - y, c)
+        if t == 0:
+            act(base)
+        else:
+            pl.when(z - t >= 0)(lambda: act(base - 4 * t))
+            pl.when(z + t <= last)(lambda: act(base + 4 * t))
+
+    start = lambda copy: copy.start()
+    keep = pltpu.make_async_copy(shard, full.at[me], local_sem)
+    spread(me, start, shard)
+    keep.start()
+
+    def arrived(j, ways):
+        whole(j, 0, right).wait_recv()
+        spread(j, start, **ways)
+
+    def across_arrived(j):
+        half(j, x, 2, across).wait_recv()
+        half(j, x, 4, peer).start()
+        half(j, x, 3, partner).start()
+
+    def peer_arrived(j):
+        half(j, 1 - x, 4, peer).wait_recv()
+        half(j, 1 - x, 3, partner).start()
+
+    for t in range(1, last + 1):
+        own_column(t, arrived)
+        other_column(t - 1, across_arrived)
+        if t > 1:
+            other_column(t - 2, peer_arrived)
+    other_column(last, across_arrived)
+    other_column(last - 1, peer_arrived)
+    other_column(last, peer_arrived)
+
+    def partner_block(i, _):
+        whole(index_of(i, y, 1 - c), 3, partner).wait_recv()
+        half(index_of(i, 1 - y, 1 - c), 0, 3, partner).wait_recv()
+        half(index_of(i, 1 - y, 1 - c), 1, 3, partner).wait_recv()
         return 0
 
-    lax.fori_loop(0, model // 128, weight_tile, 0)
-
-
-def project_kernel(width, p_own, p_east, grads, w, keep, send):
+    lax.fori_loop(0, last + 1, partner_block, 0)
+    keep.wait()
+    sent = lambda copy: copy.wait_send()
+    spread(me, sent, shard)
+    for t in range(1, last + 1):
+        own_column(t, lambda j, ways: spread(j, sent, **ways))
+
+    def other_sent(j):
+        half(j, x, 4, peer).wait_send()
+        half(j, x, 3, partner).wait_send()
+        half(j, 1 - x, 3, partner).wait_send()
+
+    for t in range(last + 1):
+        other_column(t, other_sent)
+
+
+def scatter_kernel(width, n, p_own, p_east, grads, rolled_t, w_hbm, back, out,
+                   w, mine, theirs, from_core, from_y, from_z, keep, send, west,
+                   load_sem, core_s, core_r, y_s, y_r, z_s, z_r, west_s, west_r):
+    me, z, y, c = where_am_i()
     model = w.shape[0]
-
-    def body(t, _):
+    depth = model // n
+    last = n // 4 - 1
+    load = pltpu.make_async_copy(w_hbm, w, load_sem)
+    load.start()
+    ahead = (me + 1) % n
+    barrier = pltpu.get_barrier_semaphore()
+    signal(barrier, lon=index_of(z, y, 1 - c))
+    signal(barrier, lon=index_of(z, 1 - y, c))
+    signal(barrier, lon=(me + 2 * c - 1 + n) % n)
+    pl.when(z > 0)(lambda: signal(barrier, lon=me - 4))
+    pl.when(z < last)(lambda: signal(barrier, lon=me + 4))
+    pl.semaphore_wait(barrier, 3 + line_neighbours(z, last))
+
+    def remote(src, dst, ssem, rsem, lon):
+        return pltpu.make_async_remote_copy(
+            src, dst, ssem, rsem, device_id={"lon": lon}, device_id_type=MESH)
+
+    def core_copy(k):
+        return remote(theirs.at[k], from_core.at[k], core_s.at[k], core_r.at[k], index_of(z, y, 1 - c))
+
+    def y_copy(k):
+        return remote(mine.at[k], from_y.at[k], y_s.at[k], y_r.at[k], index_of(z, 1 - y, c))
+
+    def z_copy(m, d, way):
+        to = me + 4 if way == 0 else me - 4
+        return remote(mine.at[4 + m], from_z.at[way, d], z_s.at[way, m], z_r.at[way, d], to)
+
+    def weight_block(j, dst):
+        rows = pl.ds(pl.multiple_of(j * depth, depth), depth)
+        for part, begin, end in ((0, 0, 3 * width), (1, 3 * width, 4 * width)):
+            def chunk(t, _):
+                cols = pl.ds(pl.multiple_of(t * 384, 128), 384)
+                dst[:, cols] = dot(rolled_t[part, rows, :], grads[:, cols], ((1,), (0,))).astype(bf16)
+                return 0
+            lax.fori_loop(begin // 384, end // 384, chunk, 0)
+
+    order = [3 - 3 * (z // 2), (2 + 3 * z) % 5, 1 + z % 2, z]
+
+    def add(dst, *others):
+        total = dst[...].astype(f32)
+        for other in others:
+            total += other[...].astype(f32)
+        dst[...] = total.astype(bf16)
+
+    def pass_across(k):
+        core_copy(k).wait_recv()
+        add(mine.at[k], from_core.at[k])
+        y_copy(k).start()
+
+    for k in range(8):
+        chip = order[k % 4] * 2 + (1 - y if k < 4 else y)
+        weight_block(chip * 2 + 1 - c, theirs.at[k])
+        core_copy(k).start()
+        weight_block(chip * 2 + c, mine.at[k])
+        if 1 <= k <= 4:
+            pass_across(k - 1)
+
+    load.wait()
+
+    def project(t, _):
         rows = pl.ds(pl.multiple_of(t * 256, 256), 256)
         attended = dot(grads[:, 3 * width :], w[rows, 3 * width :], ((1,), (1,))).astype(bf16)
         grad_normed = dot(grads[:, : 3 * width], w[rows, : 3 * width], ((1,), (1,))).astype(bf16)
@@ -126,7 +296,52 @@
             send[part, :, rows] = dot(p_east[...], field, ((0,), (0,))).astype(bf16)
         return 0
 
-    lax.fori_loop(0, model // 256, body, 0)
+    lax.fori_loop(0, model // 256, project, 0)
+    west_copy = remote(send, west, west_s, west_r, ahead)
+    west_copy.start()
+
+    for m in range(4):
+        d = order[m]
+        core_copy(4 + m).wait_recv()
+        y_copy(m).wait_recv()
+        add(mine.at[4 + m], from_core.at[4 + m], from_y.at[m])
+        if m < 3:
+            def go_right():
+                def more():
+                    z_copy(m, d, 0).wait_recv()
+                    add(mine.at[4 + m], from_z.at[0, d])
+                pl.when(z > 0)(more)
+                z_copy(m, d, 0).start()
+
+            def go_left():
+                def more():
+                    z_copy(m, d, 1).wait_recv()
+                    add(mine.at[4 + m], from_z.at[1, d])
+                pl.when(z < last)(more)
+                z_copy(m, d, 1).start()
+
+            pl.when(d > z)(go_right)
+            pl.when(d < z)(go_left)
+
+    west_copy.wait_recv()
+    back[...] = (keep[...].astype(f32) + west[...].astype(f32)).astype(bf16)
+    out[...] = mine[7].astype(f32)
+
+    def final(way):
+        z_copy(3, z, way).wait_recv()
+        out[...] += from_z[way, z].astype(f32)
+
+    pl.when(z > 0)(lambda: final(0))
+    pl.when(z < last)(lambda: final(1))
+    west_copy.wait_send()
+    for k in range(8):
+        core_copy(k).wait_send()
+    for k in range(4):
+        y_copy(k).wait_send()
+    for m in range(3):
+        d = order[m]
+        pl.when(d > z)(lambda: z_copy(m, d, 0).wait_send())
+        pl.when(d < z)(lambda: z_copy(m, d, 1).wait_send())
 
 
 def on_device(tokens, land, surface, gain, weights, shifts, index_table, bias_table, cotangent):
@@ -137,7 +352,22 @@
     count = levels * tile_rows * tile_cols
     area = tile_rows * tile_rows
     lats = lax.axis_size("lat")
-    w = lax.all_gather(weights, "lon", axis=0, tiled=True)
+    n = lax.axis_size("lon")
+    depth = model // n
+    dma = pltpu.SemaphoreType.DMA
+    w = pl.pallas_call(
+        functools.partial(gather_kernel, n),
+        name="gather",
+        out_shape=jax.ShapeDtypeStruct((n, 2, depth // 2, 4 * width), bf16),
+        in_specs=[VMEM],
+        out_specs=ANY,
+        scratch_shapes=[dma, dma((n, 5, 2)), dma((n, 2))],
+        compiler_params=pltpu.CompilerParams(
+            collective_id=0, has_side_effects=True, vmem_limit_bytes=8 * 2**20
+        ),
+        cost_estimate=pl.CostEstimate(flops=0, bytes_accessed=120 * 10**6, transcendentals=0),
+    )(weights.reshape(2, depth // 2, 4 * width))
+    w = w.reshape(model, 4 * width)
 
     surface_term = jnp.where(land[None, :, :, None] == 1, surface[1], surface[0])
     stream = (tokens.astype(f32) + surface_term).astype(bf16)
@@ -176,31 +406,46 @@
     )
 
     params = pltpu.CompilerParams(vmem_limit_bytes=56 * 2**20)
-    grads, dw = pl.pallas_call(
-        lambda a, b, c, d, e, f, g, h, r, p: attend_kernel(width, a, b, c, d, e, f, r, None, g, h, p),
+    grads, rolled_t = pl.pallas_call(
+        functools.partial(attend_kernel, width),
         name="attend",
         out_shape=(
             jax.ShapeDtypeStruct((count, 4 * width), bf16),
-            jax.ShapeDtypeStruct((model, 4 * width), bf16),
+            jax.ShapeDtypeStruct((2, model, count), bf16),
         ),
         in_specs=[VMEM] * 6,
         out_specs=(VMEM, VMEM),
         scratch_shapes=[pltpu.VMEM((2, count, model), bf16), pltpu.VMEM((count, 4 * width), bf16)],
         compiler_params=params,
-        cost_estimate=pl.CostEstimate(flops=3 * 10**9, bytes_accessed=24 * 10**6, transcendentals=200000),
+        cost_estimate=pl.CostEstimate(flops=3 * 10**9, bytes_accessed=15 * 10**6, transcendentals=200000),
     )(p_own, p_east, mine, east, w, bias)
-    summed = lax.psum_scatter(dw, "lon", scatter_dimension=0, tiled=True)
-    keep, send = pl.pallas_call(
-        functools.partial(project_kernel, width),
-        name="project",
-        out_shape=(jax.ShapeDtypeStruct((2, count, model), bf16),) * 2,
-        in_specs=[VMEM] * 4,
+    block = (depth, 4 * width)
+    back, summed = pl.pallas_call(
+        functools.partial(scatter_kernel, width, n),
+        name="scatter",
+        out_shape=(
+            jax.ShapeDtypeStruct((2, count, model), bf16),
+            jax.ShapeDtypeStruct(block, f32),
+        ),
+        in_specs=[VMEM] * 4 + [ANY],
         out_specs=(VMEM, VMEM),
-        compiler_params=params,
-        cost_estimate=pl.CostEstimate(flops=2 * 10**9, bytes_accessed=13 * 10**6, transcendentals=0),
-    )(p_own, p_east, grads, w)
-    west = passed_along(send, "lon", 1)
-    back = (keep.astype(f32) + west.astype(f32)).astype(bf16)
+        scratch_shapes=[
+            pltpu.VMEM((model, 4 * width), bf16),
+            pltpu.VMEM((8,) + block, bf16),
+            pltpu.VMEM((8,) + block, bf16),
+            pltpu.VMEM((8,) + block, bf16),
+            pltpu.VMEM((4,) + block, bf16),
+            pltpu.VMEM((2, 4) + block, bf16),
+            pltpu.VMEM((2, count, model), bf16),
+            pltpu.VMEM((2, count, model), bf16),
+            pltpu.VMEM((2, count, model), bf16),
+            dma, dma((8,)), dma((8,)), dma((4,)), dma((4,)), dma((2, 4)), dma((2, 4)), dma, dma,
+        ],
+        compiler_params=pltpu.CompilerParams(
+            collective_id=1, has_side_effects=True, vmem_limit_bytes=60 * 2**20
+        ),
+        cost_estimate=pl.CostEstimate(flops=3 * 10**9, bytes_accessed=150 * 10**6, transcendentals=0),
+    )(p_own, p_east, grads, rolled_t, w)
     back = back.reshape(2, levels, tile_rows, tile_cols, model)
     if lats > 1:
         above = passed_along(back, "lat", 1)
@@ -210,7 +455,8 @@
     output = (stream.astype(f32) + back[0].astype(f32)).astype(bf16)
     grad_stream = normalize_back(stream, gain, back[1])
     grad_tokens = (cotangent.astype(f32) + grad_stream).astype(bf16)
-    summed = lax.psum(summed, "lat").astype(f32)
+    if lats > 1:
+        summed = lax.psum(summed, "lat")
     token_count = count * lats * lax.axis_size("lon")
     grad_weights = summed * (1.0 / math.sqrt(token_count))
     return (output, grad_tokens, grad_weights)

time: 242 us -> 190 us (0.79)
  waiting for transfers between devices: 168 us -> 0.01 us
  Pallas kernels: 36.2 us -> 165 us
  between operations: 14.2 us -> 0.85 us
  local copies, waits for them, and re-layouts: 3.2 us -> 7.72 us
    pallas_call x2 -> x3, Pallas kernels: 36.2 us -> 165 us  [the longest x1 93.8 us: on_device(): pl.pallas_call(functools.partial(scatter_kernel, width, n), name='scatter...]
    reduce_scatter x1 -> x0, waiting for transfers between devices: 85.3 us -> none  [on_device(): summed = lax.psum_scatter(dw, 'lon', scatter_dimension=0, tiled=True)]
    all_gather x1 -> x0, waiting for transfers between devices: 66.7 us -> none  [on_device(): w = lax.all_gather(weights, 'lon', axis=0, tiled=True)]
    ppermute x2 -> x1, waiting for transfers between devices: 15.7 us -> 0.01 us  [passed_along(): lax.ppermute(shard, axis, [(i, (i + by) % count) for i in range(count)])]
    unnamed x14 -> x20, local copies, waits for them, and re-layouts: 0.03 us -> 4.55 us
  transfers between devices with their start and end apart: 4 -> 1, of which waited for: 4 -> 0; matrix products, arithmetic and copies ran while one was open for 7% -> 5% of each run, Pallas kernels for 4% -> 28%
where the time goes in v2:
time: 190 us; the launch traced here: 189 us
  Pallas kernels  165 us (87%)
  other arithmetic  11.9 us (6%)
  local copies, waits for them, and re-layouts  7.72 us (4%)
  matrix products  3.01 us (2%)
    pallas_call x1, Pallas kernels, on_device(): pl.pallas_call(functools.partial(scatter_kernel, width, n), name='scatter...  93.8 us
    pallas_call x1, Pallas kernels, on_device(): pl.pallas_call(functools.partial(gather_kernel, n), name='gather', out_sh...  52.7 us
    pallas_call x1, Pallas kernels, on_device(): pl.pallas_call(functools.partial(attend_kernel, width), name='attend', ou...  18.5 us
    unnamed x20, local copies, waits for them, and re-layouts  4.55 us
  transfers between devices with their start and end apart: 1, of which 0 were waited for; matrix products, arithmetic and copies ran while one was open for 5% of the time, Pallas kernels for 28%

profile of v2, /device:TPU:13, one launch (start us, length us, event | category | flops | bytes accessed | tf_op | source)
XLA Modules:
  0.0 189.2 jit_solution(14249142108608671183)
XLA Ops:
  0.6 0.7 broadcast_compare_fusion.1
  1.3 0.8 slice_reduce_fusion.1
  2.3 1.2 convert_reduce_fusion
  3.5 0.3 fusion.15
  3.8 0.3 fusion.9
  4.2 0.7 collective-permute-start
  4.9 0.1 subtract_reduce_fusion
  5.1 1.5 gather_fusion
  7.0 3.0 %fusion.1 = f32[64,64,2,12]{1,3,2,0:T(8,128)S(1)} fusion(s32[64,64]{1,0:T(8,128)S(1)} %copy-done.8, f32[2,225,12]{1,0,2:T(2,128)S(1)} %copy-done.9), kind=kOutput, calls=%fused_computation.3 | convolution fusion | flops 266342400 | bytes 431200 | tf_op jit(solution)/shard_map/qkr,lrh->hlqk/dot_general | solution.py:395
  10.0 0.5 bitcast_select_fusion
  10.6 1.1 pad_maximum_fusion.bias
  11.7 52.7 %gather.11 = bf16[16,2,48,3072]{3,2,1,0:T(8,128)(2,1)S(1)} custom-call(bf16[2,48,3072]{2,1,0:T(8,128)(2,1)S(1)} %bitcast.33), custom_call_target="tpu_custom_call" | custom-call | bytes 120000000 | tf_op jit(solution)/shard_map/gather/pallas_call | solution.py:358
  64.4 3.6 %copy-done = bf16[16,2,48,3072]{3,2,1,0:T(8,128)(2,1)} copy-done((bf16[16,2,48,3072]{3,2,1,0:T(8,128)(2,1)}, bf16[16,2,48,3072]{3,2,1,0:T(8,128)(2,1)S(1)}, u32[]{:S(2)}) %copy-start) | copy-done | bytes 9437208
  68.0 0.5 fusion.33
  68.5 1.3 fusion.23
  69.8 0.7 select_convert_fusion
  70.6 0.9 copy-done.6
  71.5 18.5 %attend.1 = (bf16[128,3072]{1,0:T(8,128)(2,1)}, bf16[2,1536,128]{2,1,0:T(8,128)(2,1)}) custom-call(bf16[128,128]{1,0:T(8,128)(2,1)} %get-tuple-element.26.p_own, bf16[128,128]{1,0:T(8,128)(2,1)} %get-tuple-element.25.p_east, bf16[2,128,1536]{2,1,0:T(8,128)(2,1)} %copy-done.3, bf16[2,128,1536]{2,1,0:T(8,128)(2,1)} %copy-done.6, bf16[1536,3072]{1,0:T(8,128)(2,1)} %bitcast.31, ...), custom_call_target="tpu_custom_call" | custom-call | flops 3000000000 | bytes 15000000 | tf_op jit(solution)/shard_map/attend/pallas_call | solution.py:409
  90.0 93.8 %scatter.1 = (bf16[2,128,1536]{2,1,0:T(8,128)(2,1)}, f32[96,3072]{1,0:T(8,128)}) custom-call(bf16[128,128]{1,0:T(8,128)(2,1)} %get-tuple-element.26.p_own, bf16[128,128]{1,0:T(8,128)(2,1)} %get-tuple-element.25.p_east, bf16[128,3072]{1,0:T(8,128)(2,1)} %get-tuple-element.7.grads, bf16[2,1536,128]{2,1,0:T(8,128)(2,1)} %get-tuple-element.8.rolled_t, ...), custom_call_target="tpu_custom_call" | custom-call | flops 3000000000 | bytes 150000000 | tf_op jit(solution)/shard_map/scatter/pallas_call | solution.py:423
  183.8 1.3 multiply_reduce_fusion
  185.1 1.2 slice_convert_fusion
  186.3 1.1 broadcast_multiply_fusion
  187.5 0.3 fusion.10
  187.9 1.4 fusion.14
  (34 shorter events, 0.8 us)
Async XLA Ops:
  0.6 3.1 %copy-start.7 = (f32[1536]{0:T(1024)S(1)}, f32[1536]{0:T(1024)}, u32[]{:S(2)}) copy-start(f32[1536]{0:T(1024)} %param.12) | copy-start | bytes 18436
  2.3 1.8 copy-start.4
  3.8 1.2 copy-start.2
  4.1 2.9 %copy-start.8 = (s32[64,64]{1,0:T(8,128)S(1)}, s32[64,64]{1,0:T(8,128)}, u32[]{:S(2)}) copy-start(s32[64,64]{1,0:T(8,128)} %param.15) | copy-start | bytes 49156
  4.1 2.9 %copy-start.9 = (f32[2,225,12]{1,0,2:T(2,128)S(1)}, f32[2,225,12]{1,0,2:T(2,128)}, u32[]{:S(2)}) copy-start(f32[2,225,12]{1,0,2:T(2,128)} %param.16) | copy-start | bytes 64804
  4.2 6.3 %copy-start.3 = (bf16[2,128,1536]{2,1,0:T(8,128)(2,1)}, bf16[2,128,1536]{2,1,0:T(8,128)(2,1)S(1)}, u32[]{:S(2)}) copy-start(bf16[2,128,1536]{2,1,0:T(8,128)(2,1)S(1)} %pad_maximum_fusion.1.mine) | copy-start | bytes 2359300
  4.2 66.4 %collective-permute-start = (bf16[2,128,1536]{2,1,0:T(8,128)(2,1)S(1)}, bf16[2,128,1536]{2,1,0:T(8,128)(2,1)S(1)}, u32[]{:S(2)}, u32[]{:S(2)}) collective-permute-start(bf16[2,128,1536]{2,1,0:T(8,128)(2,1)S(1)} %pad_maximum_fusion.1.mine), channel_id=1, source_target_pairs={{0,15},{1,0},{2,1},{3,2},{4,3},{5,4},{6,5},{7,6},{8,7},{9,8},{10,9... | collective-permute-start | bytes 2359304 | tf_op jit(solution)/shard_map/ppermute | solution.py:21
  10.6 1.1 copy-start.1
  64.4 3.6 %copy-start = (bf16[16,2,48,3072]{3,2,1,0:T(8,128)(2,1)}, bf16[16,2,48,3072]{3,2,1,0:T(8,128)(2,1)S(1)}, u32[]{:S(2)}) copy-start(bf16[16,2,48,3072]{3,2,1,0:T(8,128)(2,1)S(1)} %gather.11) | copy-start | bytes 28311556
  70.6 0.9 copy-start.6
  183.8 2.5 %copy-start.5 = (f32[96,3072]{1,0:T(8,128)S(1)}, f32[96,3072]{1,0:T(8,128)}, u32[]{:S(2)}) copy-start(f32[96,3072]{1,0:T(8,128)} %get-tuple-element.10) | copy-start | bytes 3538948

commit v3 on v2

--- a/solution.py
+++ b/solution.py
@@ -124,7 +124,7 @@
     return (z + last) // (last + 1) + (2 * last - z) // (last + 1)
 
 
-def gather_kernel(n, shard, full, local_sem, send_sem, recv_sem):
+def gather_kernel(n, shard, fields, full, east, local_sem, send_sem, recv_sem, halo_s, halo_r):
     me, z, y, c = where_am_i()
     x = lax.axis_index("grp")
     last = n // 4 - 1
@@ -132,9 +132,12 @@
     signal(barrier, grp=1 - x)
     signal(barrier, lon=index_of(z, y, 1 - c))
     signal(barrier, lon=index_of(z, 1 - y, c))
+    signal(barrier, lon=(me + 2 * c - 1 + n) % n)
     pl.when(z > 0)(lambda: signal(barrier, lon=me - 4))
     pl.when(z < last)(lambda: signal(barrier, lon=me + 4))
-    pl.semaphore_wait(barrier, 3 + line_neighbours(z, last))
+    pl.semaphore_wait(barrier, 4 + line_neighbours(z, last))
+    halo = pltpu.make_async_remote_copy(
+        fields, east, halo_s, halo_r, device_id={"lon": (me + n - 1) % n}, device_id_type=MESH)
 
     def whole(j, way, where, src=None):
         return pltpu.make_async_remote_copy(
@@ -178,6 +181,7 @@
     keep = pltpu.make_async_copy(shard, full.at[me], local_sem)
     spread(me, start, shard)
     keep.start()
+    halo.start()
 
     def arrived(j, ways):
         whole(j, 0, right).wait_recv()
@@ -209,6 +213,7 @@
 
     lax.fori_loop(0, last + 1, partner_block, 0)
     keep.wait()
+    halo.wait()
     sent = lambda copy: copy.wait_send()
     spread(me, sent, shard)
     for t in range(1, last + 1):
@@ -224,7 +229,7 @@
 
 
 def scatter_kernel(width, n, p_own, p_east, grads, rolled_t, w_hbm, back, out,
-                   w, mine, theirs, from_core, from_y, from_z, keep, send, west,
+                   w, blocks, from_core, from_y, from_z, keep, send, west,
                    load_sem, core_s, core_r, y_s, y_r, z_s, z_r, west_s, west_r):
     me, z, y, c = where_am_i()
     model = w.shape[0]
@@ -245,24 +250,28 @@
         return pltpu.make_async_remote_copy(
             src, dst, ssem, rsem, device_id={"lon": lon}, device_id_type=MESH)
 
+    mine = lambda k: blocks.at[k, c]
+
     def core_copy(k):
-        return remote(theirs.at[k], from_core.at[k], core_s.at[k], core_r.at[k], index_of(z, y, 1 - c))
+        return remote(blocks.at[k, 1 - c], from_core.at[k], core_s.at[k], core_r.at[k], index_of(z, y, 1 - c))
 
     def y_copy(k):
-        return remote(mine.at[k], from_y.at[k], y_s.at[k], y_r.at[k], index_of(z, 1 - y, c))
+        return remote(mine(k), from_y.at[k], y_s.at[k], y_r.at[k], index_of(z, 1 - y, c))
 
     def z_copy(m, d, way):
         to = me + 4 if way == 0 else me - 4
-        return remote(mine.at[4 + m], from_z.at[way, d], z_s.at[way, m], z_r.at[way, d], to)
-
-    def weight_block(j, dst):
-        rows = pl.ds(pl.multiple_of(j * depth, depth), depth)
+        return remote(mine(4 + m), from_z.at[way, d], z_s.at[way, m], z_r.at[way, d], to)
+
+    def weight_block(chip, k):
+        rows = pl.ds(pl.multiple_of(chip * 2 * depth, 2 * depth), 2 * depth)
         for part, begin, end in ((0, 0, 3 * width), (1, 3 * width, 4 * width)):
             def chunk(t, _):
-                cols = pl.ds(pl.multiple_of(t * 384, 128), 384)
-                dst[:, cols] = dot(rolled_t[part, rows, :], grads[:, cols], ((1,), (0,))).astype(bf16)
+                cols = pl.ds(pl.multiple_of(t * 256, 256), 256)
+                both = dot(rolled_t[part, rows, :], grads[:, cols], ((1,), (0,))).astype(bf16)
+                blocks[k, 0, :, cols] = both[:depth]
+                blocks[k, 1, :, cols] = both[depth:]
                 return 0
-            lax.fori_loop(begin // 384, end // 384, chunk, 0)
+            lax.fori_loop(begin // 256, end // 256, chunk, 0)
 
     order = [3 - 3 * (z // 2), (2 + 3 * z) % 5, 1 + z % 2, z]
 
@@ -274,18 +283,15 @@
 
     def pass_across(k):
         core_copy(k).wait_recv()
-        add(mine.at[k], from_core.at[k])
+        add(mine(k), from_core.at[k])
         y_copy(k).start()
 
-    for k in range(8):
+    def block_step(k):
         chip = order[k % 4] * 2 + (1 - y if k < 4 else y)
-        weight_block(chip * 2 + 1 - c, theirs.at[k])
+        weight_block(chip, k)
         core_copy(k).start()
-        weight_block(chip * 2 + c, mine.at[k])
         if 1 <= k <= 4:
             pass_across(k - 1)
-
-    load.wait()
 
     def project(t, _):
         rows = pl.ds(pl.multiple_of(t * 256, 256), 256)
@@ -296,36 +302,52 @@
             send[part, :, rows] = dot(p_east[...], field, ((0,), (0,))).astype(bf16)
         return 0
 
-    lax.fori_loop(0, model // 256, project, 0)
     west_copy = remote(send, west, west_s, west_r, ahead)
-    west_copy.start()
-
-    for m in range(4):
+
+    def project_all():
+        load.wait()
+        lax.fori_loop(0, model // 256, project, 0)
+        west_copy.start()
+
+    inner = (z + 1) // 2 % 2
+
+    def line_step(m):
         d = order[m]
         core_copy(4 + m).wait_recv()
         y_copy(m).wait_recv()
-        add(mine.at[4 + m], from_core.at[4 + m], from_y.at[m])
+        add(mine(4 + m), from_core.at[4 + m], from_y.at[m])
         if m < 3:
             def go_right():
                 def more():
                     z_copy(m, d, 0).wait_recv()
-                    add(mine.at[4 + m], from_z.at[0, d])
+                    add(mine(4 + m), from_z.at[0, d])
                 pl.when(z > 0)(more)
                 z_copy(m, d, 0).start()
 
             def go_left():
                 def more():
                     z_copy(m, d, 1).wait_recv()
-                    add(mine.at[4 + m], from_z.at[1, d])
+                    add(mine(4 + m), from_z.at[1, d])
                 pl.when(z < last)(more)
                 z_copy(m, d, 1).start()
 
             pl.when(d > z)(go_right)
             pl.when(d < z)(go_left)
 
+    for k in range(5):
+        block_step(k)
+    pl.when(inner == 1)(project_all)
+    line_step(0)
+    block_step(5)
+    pl.when(inner == 0)(project_all)
+    line_step(1)
+    block_step(6)
+    block_step(7)
+    line_step(2)
+    line_step(3)
     west_copy.wait_recv()
     back[...] = (keep[...].astype(f32) + west[...].astype(f32)).astype(bf16)
-    out[...] = mine[7].astype(f32)
+    out[...] = blocks[7, c].astype(f32)
 
     def final(way):
         z_copy(3, z, way).wait_recv()
@@ -355,19 +377,6 @@
     n = lax.axis_size("lon")
     depth = model // n
     dma = pltpu.SemaphoreType.DMA
-    w = pl.pallas_call(
-        functools.partial(gather_kernel, n),
-        name="gather",
-        out_shape=jax.ShapeDtypeStruct((n, 2, depth // 2, 4 * width), bf16),
-        in_specs=[VMEM],
-        out_specs=ANY,
-        scratch_shapes=[dma, dma((n, 5, 2)), dma((n, 2))],
-        compiler_params=pltpu.CompilerParams(
-            collective_id=0, has_side_effects=True, vmem_limit_bytes=8 * 2**20
-        ),
-        cost_estimate=pl.CostEstimate(flops=0, bytes_accessed=120 * 10**6, transcendentals=0),
-    )(weights.reshape(2, depth // 2, 4 * width))
-    w = w.reshape(model, 4 * width)
 
     surface_term = jnp.where(land[None, :, :, None] == 1, surface[1], surface[0])
     stream = (tokens.astype(f32) + surface_term).astype(bf16)
@@ -379,7 +388,22 @@
         fields = jax.vmap(lambda f: take_levels(f[None], row_shift, 2, tile_rows)[0])(both)
         row_shift = jnp.zeros_like(row_shift)
     mine = fields.reshape(2, count, model)
-    east = passed_along(mine, "lon", -1)
+    w, east = pl.pallas_call(
+        functools.partial(gather_kernel, n),
+        name="gather",
+        out_shape=(
+            jax.ShapeDtypeStruct((n, 2, depth // 2, 4 * width), bf16),
+            jax.ShapeDtypeStruct((2, count, model), bf16),
+        ),
+        in_specs=[VMEM, VMEM],
+        out_specs=(ANY, ANY),
+        scratch_shapes=[dma, dma((n, 5, 2)), dma((n, 2)), dma, dma],
+        compiler_params=pltpu.CompilerParams(
+            collective_id=0, has_side_effects=True, vmem_limit_bytes=60 * 2**20
+        ),
+        cost_estimate=pl.CostEstimate(flops=0, bytes_accessed=120 * 10**6, transcendentals=0),
+    )(weights.reshape(2, depth // 2, 4 * width), mine)
+    w = w.reshape(model, 4 * width)
 
     cell = jnp.arange(count, dtype=jnp.int32)
     lev, row, col = cell // (tile_rows * tile_cols), cell // tile_cols % tile_rows, cell % tile_cols
@@ -431,8 +455,7 @@
         out_specs=(VMEM, VMEM),
         scratch_shapes=[
             pltpu.VMEM((model, 4 * width), bf16),
-            pltpu.VMEM((8,) + block, bf16),
-            pltpu.VMEM((8,) + block, bf16),
+            pltpu.VMEM((8, 2) + block, bf16),
             pltpu.VMEM((8,) + block, bf16),
             pltpu.VMEM((4,) + block, bf16),
             pltpu.VMEM((2, 4) + block, bf16),

time: 190 us -> 187 us (0.984)
  local copies, waits for them, and re-layouts: 7.72 us -> 4.49 us
    unnamed x20 -> x12, local copies, waits for them, and re-layouts: 4.55 us -> 0.26 us
    pallas_call x1, Pallas kernels: 52.7 us -> 56.3 us  [on_device(): pl.pallas_call(functools.partial(gather_kernel, n), name='gather', out_sh...]
    pallas_call x1, Pallas kernels: 93.8 us -> 90.7 us  [on_device(): pl.pallas_call(functools.partial(scatter_kernel, width, n), name='scatter...]
  transfers between devices with their start and end apart: 1 -> 0, of which waited for: 0 -> 0; matrix products, arithmetic and copies ran while one was open for 5% -> 0% of each run, Pallas kernels for 28% -> 0%
where the time goes in v3:
time: 187 us; the launch traced here: 185 us
  Pallas kernels  165 us (88%)
  other arithmetic  11.6 us (6%)
  local copies, waits for them, and re-layouts  4.49 us (2%)
  matrix products  3 us (2%)
    pallas_call x1, Pallas kernels, on_device(): pl.pallas_call(functools.partial(scatter_kernel, width, n), name='scatter...  90.7 us
    pallas_call x1, Pallas kernels, on_device(): pl.pallas_call(functools.partial(gather_kernel, n), name='gather', out_sh...  56.3 us
    pallas_call x1, Pallas kernels, on_device(): pl.pallas_call(functools.partial(attend_kernel, width), name='attend', ou...  18.5 us

profile of v3, /device:TPU:13, one launch (start us, length us, event | category | flops | bytes accessed | tf_op | source)
XLA Modules:
  0.0 185.3 jit_solution(3653202894726661905)
XLA Ops:
  0.6 0.8 subtract_reduce_fusion
  1.6 1.8 gather_fusion
  3.4 0.7 broadcast_compare_fusion.1
  4.1 1.3 fusion.33
  5.4 1.3 fusion.23
  7.0 0.8 slice_reduce_fusion.1
  7.8 0.7 select_convert_fusion
  8.5 0.1 broadcast_select_fusion
  8.7 0.2 convert_reduce_fusion
  8.8 0.3 fusion.15
  9.1 0.3 fusion.9
  9.4 0.2 copy-done.1
  9.7 0.9 pad_maximum_fusion.1.fields.mine
  10.6 3.0 %fusion.1 = f32[64,64,2,12]{1,3,2,0:T(8,128)S(1)} fusion(s32[64,64]{1,0:T(8,128)S(1)} %copy-done.4, f32[2,225,12]{1,0,2:T(2,128)S(1)} %copy-done.5), kind=kOutput, calls=%fused_computation.3 | convolution fusion | flops 266342400 | bytes 431200 | tf_op jit(solution)/shard_map/qkr,lrh->hlqk/dot_general | solution.py:419
  13.6 0.5 bitcast_select_fusion
  14.2 1.1 pad_maximum_fusion.bias
  15.3 56.3 %gather.11 = (bf16[16,2,48,3072]{3,2,1,0:T(8,128)(2,1)}, bf16[2,128,1536]{2,1,0:T(8,128)(2,1)}) custom-call(bf16[2,48,3072]{2,1,0:T(8,128)(2,1)} %bitcast.38, bf16[2,128,1536]{2,1,0:T(8,128)(2,1)} %pad_maximum_fusion.1.fields.mine), custom_call_target="tpu_custom_call" | custom-call | bytes 120000000 | tf_op jit(solution)/shard_map/gather/pallas_call | solution.py:391
  71.6 18.5 %attend.1 = (bf16[128,3072]{1,0:T(8,128)(2,1)}, bf16[2,1536,128]{2,1,0:T(8,128)(2,1)}) custom-call(bf16[128,128]{1,0:T(8,128)(2,1)} %get-tuple-element.30.p_own, bf16[128,128]{1,0:T(8,128)(2,1)} %get-tuple-element.29.p_east, bf16[2,128,1536]{2,1,0:T(8,128)(2,1)} %pad_maximum_fusion.1.fields.mine, bf16[2,128,1536]{2,1,0:T(8,128)(2,1)} %get-tuple-element.9.east, ...), custom_call_target="tpu_custom_call" | custom-call | flops 3000000000 | bytes 15000000 | tf_op jit(solution)/shard_map/attend/pallas_call | solution.py:433
  90.1 90.7 %scatter.1 = (bf16[2,128,1536]{2,1,0:T(8,128)(2,1)}, f32[96,3072]{1,0:T(8,128)}) custom-call(bf16[128,128]{1,0:T(8,128)(2,1)} %get-tuple-element.30.p_own, bf16[128,128]{1,0:T(8,128)(2,1)} %get-tuple-element.29.p_east, bf16[128,3072]{1,0:T(8,128)(2,1)} %get-tuple-element.11.grads, bf16[2,1536,128]{2,1,0:T(8,128)(2,1)} %get-tuple-element.12.rolled_t, ...), custom_call_target="tpu_custom_call" | custom-call | flops 3000000000 | bytes 150000000 | tf_op jit(solution)/shard_map/scatter/pallas_call | solution.py:447
  180.8 2.5 %broadcast_multiply_fusion = f32[96,3072]{1,0:T(8,128)} fusion(f32[96,3072]{1,0:T(8,128)} %get-tuple-element.14), kind=kLoop, calls=%fused_computation.26 | loop fusion | flops 294912 | bytes 2359296 | tf_op jit(solution)/shard_map/mul | solution.py:484
  183.2 0.2 multiply_reduce_fusion
  183.5 0.1 slice_convert_fusion
  183.6 0.3 fusion.10
  183.9 1.4 fusion.14
  (24 shorter events, 0.6 us)
Async XLA Ops:
  0.6 8.0 %copy-start.2 = (bf16[2,8,8,1536]{3,2,1,0:T(8,128)(2,1)S(1)}, bf16[2,8,8,1536]{3,2,1,0:T(8,128)(2,1)}, u32[]{:S(2)}) copy-start(bf16[2,8,8,1536]{3,2,1,0:T(8,128)(2,1)} %param.9) | copy-start | bytes 1179652
  3.4 5.7 %copy-start.3 = (f32[1536]{0:T(1024)S(1)}, f32[1536]{0:T(1024)}, u32[]{:S(2)}) copy-start(f32[1536]{0:T(1024)} %param.12) | copy-start | bytes 18436
  8.7 1.0 copy-start.1
  9.1 1.5 copy-start.4
  9.1 1.5 copy-start.5
  180.7 2.5 %copy-start = (bf16[2,128,1536]{2,1,0:T(8,128)(2,1)S(1)}, bf16[2,128,1536]{2,1,0:T(8,128)(2,1)}, u32[]{:S(2)}) copy-start(bf16[2,128,1536]{2,1,0:T(8,128)(2,1)} %get-tuple-element.13) | copy-start | bytes 2359300

commit v4 on v3

--- a/solution.py
+++ b/solution.py
@@ -139,11 +139,6 @@
     halo = pltpu.make_async_remote_copy(
         fields, east, halo_s, halo_r, device_id={"lon": (me + n - 1) % n}, device_id_type=MESH)
 
-    def whole(j, way, where, src=None):
-        return pltpu.make_async_remote_copy(
-            full.at[j] if src is None else src, full.at[j],
-            send_sem.at[j, way, 0], recv_sem.at[j, 0], device_id=where, device_id_type=MESH)
-
     def half(j, h, way, where, src=None):
         return pltpu.make_async_remote_copy(
             full.at[j, h] if src is None else src, full.at[j, h],
@@ -153,13 +148,17 @@
     across = {"lon": index_of(z, 1 - y, c)}
     right, left, peer = {"lon": me + 4}, {"lon": me - 4}, {"grp": 1 - x}
 
-    def spread(j, act, src=None, to_right=True, to_left=True):
+    halves = ((x, True), (1 - x, False))
+
+    def spread(j, act, h, first, src=None, to_right=True, to_left=True):
+        src = None if src is None else src.at[h]
         if to_right:
-            pl.when(z < last)(lambda: act(whole(j, 0, right, src)))
+            pl.when(z < last)(lambda: act(half(j, h, 0, right, src)))
         if to_left:
-            pl.when(z > 0)(lambda: act(whole(j, 1, left, src)))
-        act(half(j, x, 2, across, None if src is None else src.at[x]))
-        act(whole(j, 3, partner, src))
+            pl.when(z > 0)(lambda: act(half(j, h, 1, left, src)))
+        if first:
+            act(half(j, h, 2, across, src))
+        act(half(j, h, 3, partner, src))
 
     def own_column(t, act):
         def from_left():
@@ -179,13 +178,15 @@
 
     start = lambda copy: copy.start()
     keep = pltpu.make_async_copy(shard, full.at[me], local_sem)
-    spread(me, start, shard)
+    for h, first in halves:
+        spread(me, start, h, first, shard)
     keep.start()
     halo.start()
 
     def arrived(j, ways):
-        whole(j, 0, right).wait_recv()
-        spread(j, start, **ways)
+        for h, first in halves:
+            half(j, h, 0, right).wait_recv()
+            spread(j, start, h, first, **ways)
 
     def across_arrived(j):
         half(j, x, 2, across).wait_recv()
@@ -206,18 +207,19 @@
     other_column(last, peer_arrived)
 
     def partner_block(i, _):
-        whole(index_of(i, y, 1 - c), 3, partner).wait_recv()
-        half(index_of(i, 1 - y, 1 - c), 0, 3, partner).wait_recv()
-        half(index_of(i, 1 - y, 1 - c), 1, 3, partner).wait_recv()
+        for h in range(2):
+            half(index_of(i, y, 1 - c), h, 3, partner).wait_recv()
+            half(index_of(i, 1 - y, 1 - c), h, 3, partner).wait_recv()
         return 0
 
     lax.fori_loop(0, last + 1, partner_block, 0)
     keep.wait()
     halo.wait()
     sent = lambda copy: copy.wait_send()
-    spread(me, sent, shard)
-    for t in range(1, last + 1):
-        own_column(t, lambda j, ways: spread(j, sent, **ways))
+    for h, first in halves:
+        spread(me, sent, h, first, shard)
+        for t in range(1, last + 1):
+            own_column(t, lambda j, ways: spread(j, sent, h, first, **ways))
 
     def other_sent(j):
         half(j, x, 4, peer).wait_send()

time: 187 us -> 184 us (0.984)
  Pallas kernels: 165 us -> 162 us
    pallas_call x1, Pallas kernels: 90.7 us -> 87.8 us  [on_device(): pl.pallas_call(functools.partial(scatter_kernel, width, n), name='scatter...]
where the time goes in v4:
time: 184 us; the launch traced here: 182 us
  Pallas kernels  162 us (88%)
  other arithmetic  11.6 us (6%)
  local copies, waits for them, and re-layouts  4.49 us (2%)
  matrix products  3 us (2%)
    pallas_call x1, Pallas kernels, on_device(): pl.pallas_call(functools.partial(scatter_kernel, width, n), name='scatter...  87.8 us
    pallas_call x1, Pallas kernels, on_device(): pl.pallas_call(functools.partial(gather_kernel, n), name='gather', out_sh...  55.6 us
    pallas_call x1, Pallas kernels, on_device(): pl.pallas_call(functools.partial(attend_kernel, width), name='attend', ou...  18.5 us

profile of v4, /device:TPU:13, one launch (start us, length us, event | category | flops | bytes accessed | tf_op | source)
XLA Modules:
  0.0 181.8 jit_solution(10135046774737748581)
XLA Ops:
  0.6 0.8 subtract_reduce_fusion
  1.6 1.8 %gather_fusion = s32[128]{0:T(128)S(1)} fusion(s32[2,2]{1,0:T(2,128)} %param.14, s32[128]{0:T(128)S(1)} %or_bitcast_fusion), kind=kCustom, calls=%fused_computation | custom fusion | bytes 2048 | tf_op jit(solution)/shard_map/gather | solution.py:413
  3.4 0.7 broadcast_compare_fusion.1
  4.1 1.3 fusion.33
  5.4 1.3 fusion.23
  7.0 0.8 slice_reduce_fusion.1
  7.8 0.7 select_convert_fusion
  8.5 0.1 broadcast_select_fusion
  8.7 0.2 convert_reduce_fusion
  8.8 0.3 fusion.15
  9.1 0.3 fusion.9
  9.4 0.2 copy-done.1
  9.7 0.9 pad_maximum_fusion.1.fields.mine
  10.6 3.0 %fusion.1 = f32[64,64,2,12]{1,3,2,0:T(8,128)S(1)} fusion(s32[64,64]{1,0:T(8,128)S(1)} %copy-done.4, f32[2,225,12]{1,0,2:T(2,128)S(1)} %copy-done.5), kind=kOutput, calls=%fused_computation.3 | convolution fusion | flops 266342400 | bytes 431200 | tf_op jit(solution)/shard_map/qkr,lrh->hlqk/dot_general | solution.py:421
  13.6 0.5 bitcast_select_fusion
  14.2 1.1 pad_maximum_fusion.bias
  15.3 55.6 %gather.11 = (bf16[16,2,48,3072]{3,2,1,0:T(8,128)(2,1)}, bf16[2,128,1536]{2,1,0:T(8,128)(2,1)}) custom-call(bf16[2,48,3072]{2,1,0:T(8,128)(2,1)} %bitcast.38, bf16[2,128,1536]{2,1,0:T(8,128)(2,1)} %pad_maximum_fusion.1.fields.mine), custom_call_target="tpu_custom_call" | custom-call | bytes 120000000 | tf_op jit(solution)/shard_map/gather/pallas_call | solution.py:393
  70.9 18.5 %attend.1 = (bf16[128,3072]{1,0:T(8,128)(2,1)}, bf16[2,1536,128]{2,1,0:T(8,128)(2,1)}) custom-call(bf16[128,128]{1,0:T(8,128)(2,1)} %get-tuple-element.30.p_own, bf16[128,128]{1,0:T(8,128)(2,1)} %get-tuple-element.29.p_east, bf16[2,128,1536]{2,1,0:T(8,128)(2,1)} %pad_maximum_fusion.1.fields.mine, bf16[2,128,1536]{2,1,0:T(8,128)(2,1)} %get-tuple-element.9.east, ...), custom_call_target="tpu_custom_call" | custom-call | flops 3000000000 | bytes 15000000 | tf_op jit(solution)/shard_map/attend/pallas_call | solution.py:435
  89.5 87.8 %scatter.1 = (bf16[2,128,1536]{2,1,0:T(8,128)(2,1)}, f32[96,3072]{1,0:T(8,128)}) custom-call(bf16[128,128]{1,0:T(8,128)(2,1)} %get-tuple-element.30.p_own, bf16[128,128]{1,0:T(8,128)(2,1)} %get-tuple-element.29.p_east, bf16[128,3072]{1,0:T(8,128)(2,1)} %get-tuple-element.11.grads, bf16[2,1536,128]{2,1,0:T(8,128)(2,1)} %get-tuple-element.12.rolled_t, ...), custom_call_target="tpu_custom_call" | custom-call | flops 3000000000 | bytes 150000000 | tf_op jit(solution)/shard_map/scatter/pallas_call | solution.py:449
  177.3 2.5 %broadcast_multiply_fusion = f32[96,3072]{1,0:T(8,128)} fusion(f32[96,3072]{1,0:T(8,128)} %get-tuple-element.14), kind=kLoop, calls=%fused_computation.26 | loop fusion | flops 294912 | bytes 2359296 | tf_op jit(solution)/shard_map/mul | solution.py:486
  179.7 0.2 multiply_reduce_fusion
  180.0 0.1 slice_convert_fusion
  180.1 0.3 fusion.10
  180.5 1.4 fusion.14
  (24 shorter events, 0.6 us)
Async XLA Ops:
  0.6 8.0 %copy-start.2 = (bf16[2,8,8,1536]{3,2,1,0:T(8,128)(2,1)S(1)}, bf16[2,8,8,1536]{3,2,1,0:T(8,128)(2,1)}, u32[]{:S(2)}) copy-start(bf16[2,8,8,1536]{3,2,1,0:T(8,128)(2,1)} %param.9) | copy-start | bytes 1179652
  3.4 5.7 %copy-start.3 = (f32[1536]{0:T(1024)S(1)}, f32[1536]{0:T(1024)}, u32[]{:S(2)}) copy-start(f32[1536]{0:T(1024)} %param.12) | copy-start | bytes 18436
  8.7 1.0 copy-start.1
  9.1 1.5 copy-start.4
  9.1 1.5 copy-start.5
  177.3 2.5 %copy-start = (bf16[2,128,1536]{2,1,0:T(8,128)(2,1)S(1)}, bf16[2,128,1536]{2,1,0:T(8,128)(2,1)}, u32[]{:S(2)}) copy-start(bf16[2,128,1536]{2,1,0:T(8,128)(2,1)} %get-tuple-element.13) | copy-start | bytes 2359300
